TPU v7x, 256 devices: a whole 4x4x8 slice. The times are simulated.
256 devices in a mesh: expert: 8 (over z), tp: 8 (over x, core), dp: 4 (over y).
Axes of the slice: x: 4, y: 4, z: 8, core: 2. Of those that a mesh axis runs over, the one named last changes fastest.
Arguments:
- hidden: bfloat16 [1024, 6144], P(('expert', 'tp', 'dp')), may hold values from -400 to 400
- norm_gain: float32 [6144], replicated, may hold values from 0.1 to 1.9
- expert_ids: int32 [1024, 2], P(('expert', 'tp', 'dp')), may hold values from 0 to 7, all different within a row; in each aligned block of 4 rows (0 to 3, 4 to 7, ...) at most 2 rows name the same one
- router_logits: float32 [1024, 2], P(('expert', 'tp', 'dp')), may hold values from -6 to 6
- w_gate: bfloat16 [8, 6144, 8192], P('expert', None, ('tp', 'dp')), may hold values from -0.078125 to 0.078125
- w_up: bfloat16 [8, 6144, 8192], P('expert', None, ('tp', 'dp')), may hold values from -0.078125 to 0.078125
- w_down: bfloat16 [8, 8192, 6144], P('expert', ('tp', 'dp')), may hold values from -0.0625 to 0.0625
Outputs:
- moe_out: bfloat16 [1024, 6144], P(('expert', 'tp', 'dp'))
Inputs may be any that keep to these rules, and one draw needn't show every extreme that they name: `expert_ids`: each token names two different experts; the tokens of one device name one expert at most 2 times.
All inputs are finite; a program needn't handle non-finite values.
Results may differ from a plain program's by a relative error of at most 0.015.
Values may be sent and summed in bfloat16 or wider, within the bound.
No kernel may reach another device: no remote copies, remote signals or barrier semaphores. Data moves between devices by JAX's collectives and lax.ppermute only.
A program may use at most 64 MiB of HBM per device.

v0:
```python
import jax
import jax.numpy as jnp
from jax import lax
from jax.sharding import PartitionSpec as P


MOST = 2
PLANE = ("tp", "dp")


def plane_pairs(n_tp, n_dp, step):
    n_x = n_tp // 2
    pairs = []
    for tp in range(n_tp):
        for y in range(n_dp):
            to_x, to_y, to_core = step(tp // 2, y, tp % 2)
            target = (to_x % n_x * 2 + to_core) * n_dp + to_y % n_dp
            pairs.append((tp * n_dp + y, target))
    return pairs


def first_ring(k):
    return lambda x, y, c: (x + k * c, y + k * (1 - c), c)


def second_ring(k):
    return lambda x, y, c: (x + k * (1 - c), y + k * c, c)


def layer(hidden, norm_gain, expert_ids, router_logits, w_gate, w_up, w_down):
    width = hidden.shape[1]
    half = width // 2
    n_tp, n_dp = lax.axis_size("tp"), lax.axis_size("dp")
    core = lax.axis_index("tp") % 2
    low = core == 0

    def move(value, step):
        return lax.ppermute(value, PLANE, plane_pairs(n_tp, n_dp, step))

    def swap(value):
        return move(value, lambda x, y, c: (x, y, 1 - c))

    def own_half(value):
        return jnp.where(low, value[..., :half], value[..., half:])

    def other_half(value):
        return jnp.where(low, value[..., half:], value[..., :half])

    def joined(own, other):
        return jnp.where(
            low, jnp.concatenate([own, other], axis=-1), jnp.concatenate([other, own], axis=-1)
        )

    values = hidden.astype(jnp.float32)
    inverse = lax.rsqrt(jnp.mean(values * values, axis=1, keepdims=True) + 1e-05)
    normed = (values * inverse * norm_gain[None, :]).astype(jnp.bfloat16)
    groups = lax.axis_size("expert")
    assigned = expert_ids.reshape(-1)
    onehot = (assigned[:, None] == jnp.arange(groups, dtype=jnp.int32)[None, :]).astype(jnp.int32)
    earlier = jnp.cumsum(onehot, axis=0) - onehot
    position = jnp.sum(earlier * onehot, axis=1)
    chosen = assigned[None, None, :] == jnp.arange(groups, dtype=jnp.int32)[:, None, None]
    placed = position[None, None, :] == jnp.arange(MOST, dtype=jnp.int32)[None, :, None]
    selector = (chosen & placed).astype(jnp.bfloat16).reshape(groups * MOST, assigned.shape[0])
    repeated = jnp.repeat(normed, 2, axis=0)
    bucket = jnp.dot(selector, repeated, preferred_element_type=jnp.float32).astype(jnp.bfloat16)
    arrived = lax.all_to_all(
        bucket.reshape(groups, MOST, width), "expert", split_axis=0, concat_axis=0, tiled=True
    )
    arrived = arrived.reshape(groups * MOST, width)
    rows = groups * MOST

    mine = own_half(arrived)
    theirs = swap(other_half(arrived))
    pair = jnp.where(
        low, jnp.concatenate([mine, theirs], axis=0), jnp.concatenate([theirs, mine], axis=0)
    )
    line = jnp.concatenate(
        [pair, move(pair, first_ring(-1)), move(pair, first_ring(1)), move(pair, first_ring(2))],
        axis=0,
    )
    line_rows = line.shape[0]
    cut = line_rows // 2
    ahead, back = second_ring(1), second_ring(-1)

    before_top = move(line[:cut], ahead)
    after_bottom = move(line[cut:], back)
    after_top = move(line[:cut], back)
    before_bottom = move(line[cut:], ahead)
    far_top = move(before_top, ahead)
    far_bottom = move(after_bottom, back)
    own_x = [
        line,
        jnp.concatenate([after_top, after_bottom], axis=0),
        jnp.concatenate([before_top, before_bottom], axis=0),
        jnp.concatenate([far_top, far_bottom], axis=0),
    ]
    other_x = [swap(block) for block in own_x]

    def reordered(value):
        blocks = value.reshape(4, 4, 2 * rows, value.shape[-1])
        return jnp.swapaxes(blocks, 0, 1).reshape(value.shape)

    def both_halves(matrix):
        own = lax.dynamic_slice_in_dim(matrix, core * half, half, 0)
        other = lax.dynamic_slice_in_dim(matrix, (1 - core) * half, half, 0)

        def product(block, part):
            return jnp.dot(block, part, preferred_element_type=jnp.float32)

        own = [product(own_x[i], own) for i in range(4)]
        other = [product(other_x[i], other) for i in range(4)]
        return jnp.concatenate(own, axis=0) + reordered(jnp.concatenate(other, axis=0))

    gate_val, up_val = both_halves(w_gate[0]), both_halves(w_up[0])
    activations = (jax.nn.silu(gate_val) * up_val).astype(jnp.bfloat16)
    for_partner = reordered(activations).reshape(4, line_rows, -1)
    activations = activations.reshape(4, line_rows, -1)
    down_own = lax.dynamic_slice_in_dim(w_down[0], core * half, half, 1)
    down_other = lax.dynamic_slice_in_dim(w_down[0], (1 - core) * half, half, 1)

    def add(*terms):
        result = terms[0].astype(jnp.float32)
        for term in terms[1:]:
            result = result + term.astype(jnp.float32)
        return result

    def down(block):
        given = jnp.dot(for_partner[block], down_other, preferred_element_type=jnp.float32)
        given = swap(given.astype(jnp.bfloat16))
        kept = jnp.dot(activations[block], down_own, preferred_element_type=jnp.float32)
        return add(kept.astype(jnp.bfloat16), given)

    low_type = jnp.bfloat16
    to_far = down(3).astype(low_type)
    through_top = move(to_far[:cut], ahead)
    through_bottom = move(to_far[cut:], back)
    to_after = down(1)
    to_before = down(2)
    from_before_bottom = move(to_after[cut:].astype(low_type), ahead)
    from_after_top = move(to_before[:cut].astype(low_type), back)
    from_before_top = move(add(to_after[:cut], through_top).astype(low_type), ahead)
    from_after_bottom = move(add(to_before[cut:], through_bottom).astype(low_type), back)
    kept = down(0)
    line_sum = jnp.concatenate(
        [
            add(kept[:cut], from_before_top, from_after_top),
            add(kept[cut:], from_before_bottom, from_after_bottom),
        ],
        axis=0,
    ).astype(low_type)
    line_sum = line_sum.reshape(4, 2 * rows, half)
    pair_sum = add(
        line_sum[0],
        move(line_sum[1], first_ring(1)),
        move(line_sum[2], first_ring(-1)),
        move(line_sum[3], first_ring(2)),
    ).astype(jnp.bfloat16)
    mine = jnp.where(low, pair_sum[:rows], pair_sum[rows:])
    theirs = swap(jnp.where(low, pair_sum[rows:], pair_sum[:rows]))
    summed = joined(mine, theirs)

    outgoing = summed.reshape(groups, MOST, width)
    returned = lax.all_to_all(outgoing, "expert", split_axis=0, concat_axis=0, tiled=True)
    picked = jnp.dot(
        selector.T, returned.reshape(groups * MOST, width), preferred_element_type=jnp.float32
    )
    picked = picked.reshape(hidden.shape[0], 2, width)
    first = jax.nn.sigmoid(router_logits[:, 0] - router_logits[:, 1])
    second = jax.nn.sigmoid(router_logits[:, 1] - router_logits[:, 0])
    route_weight = jnp.stack([first, second], axis=1)
    combined = jnp.sum(picked * route_weight[:, :, None], axis=1)
    return combined.astype(jnp.bfloat16)


def solution(mesh):
    placed = (
        P(("expert", "tp", "dp"), None),
        P(),
        P(("expert", "tp", "dp"), None),
        P(("expert", "tp", "dp"), None),
        P("expert", None, ("tp", "dp")),
        P("expert", None, ("tp", "dp")),
        P("expert", ("tp", "dp"), None),
    )
    return jax.shard_map(
        layer, mesh=mesh, in_specs=placed, out_specs=P(("expert", "tp", "dp"), None), check_vma=False
    )
```

profile of v0, /device:TPU:6, one launch (start us, length us, event | category | flops | bytes accessed | tf_op | source)
XLA Modules:
  0.0 119.3 jit_solution(13764224708512538822)
XLA Ops:
  4.3 8.5 %all-to-all-start = ((bf16[8,2,6144]{2,1,0:T(2,128)(2,1)}), bf16[8,2,6144]{2,1,0:T(2,128)(2,1)S(1)}, u32[]{:S(2)}, u32[]{:S(2)}) async-start(bf16[8,2,6144]{2,1,0:T(2,128)(2,1)} %reshape.141), calls=%async_computation | async-start | bytes 393216 | tf_op jit(solution)/shard_map/all_to_all | solution.py:67
  12.8 10.5 %all-to-all-done = bf16[8,2,6144]{2,1,0:T(2,128)(2,1)S(1)} async-done(((bf16[8,2,6144]{2,1,0:T(2,128)(2,1)}), bf16[8,2,6144]{2,1,0:T(2,128)(2,1)S(1)}, u32[]{:S(2)}, u32[]{:S(2)}) %all-to-all-start) | async-done | bytes 196640 | tf_op jit(solution)/shard_map/all_to_all | solution.py:67
  24.8 1.7 %collective-permute-start.2 = (bf16[32,3072]{1,0:T(8,128)(2,1)S(1)}, bf16[32,3072]{1,0:T(8,128)(2,1)S(1)}, u32[]{:S(2)}, u32[]{:S(2)}) collective-permute-start(bf16[32,3072]{1,0:T(8,128)(2,1)S(1)} %maximum_select_fusion), channel_id=1, source_target_pairs={{0,1},{1,2},{2,3},{3,0},{4,12},{5,13},{6,14},{7,15},{8,9},{9,10},{... | collective-permute-start | bytes 589832 | tf_op jit(solution)/shard_map/ppermute | solution.py:38
  26.5 2.9 %collective-permute-start.3 = (bf16[32,3072]{1,0:T(8,128)(2,1)S(1)}, bf16[32,3072]{1,0:T(8,128)(2,1)S(1)}, u32[]{:S(2)}, u32[]{:S(2)}) collective-permute-start(bf16[32,3072]{1,0:T(8,128)(2,1)S(1)} %maximum_select_fusion), channel_id=1, source_target_pairs={{0,2},{1,3},{2,0},{3,1},{4,20},{5,21},{6,22},{7,23},{8,10},{9,11},... | collective-permute-start | bytes 589832 | tf_op jit(solution)/shard_map/ppermute | solution.py:38
  31.8 3.3 %collective-permute-done.3 = bf16[32,3072]{1,0:T(8,128)(2,1)S(1)} collective-permute-done((bf16[32,3072]{1,0:T(8,128)(2,1)S(1)}, bf16[32,3072]{1,0:T(8,128)(2,1)S(1)}, u32[]{:S(2)}, u32[]{:S(2)}) %collective-permute-start.3) | collective-permute-done | bytes 196640 | tf_op jit(solution)/shard_map/ppermute | solution.py:38
  35.7 1.5 %collective-permute-start.5 = (bf16[64,3072]{1,0:T(8,128)(2,1)S(1)}, bf16[64,3072]{1,0:T(8,128)(2,1)S(1)}, u32[]{:S(2)}, u32[]{:S(2)}) collective-permute-start(bf16[64,3072]{1,0:T(8,128)(2,1)S(1)} %constant_dynamic-update-slice_fusion), channel_id=1, source_target_pairs={{0,24},{1,25},{2,26},{3,27},{4,7},{5,4},{6,5},{7,6},{8,0},{9,1},{1... | collective-permute-start | bytes 1179656 | tf_op jit(solution)/shard_map/ppermute | solution.py:38
  37.3 1.8 %collective-permute-start.6 = (bf16[64,3072]{1,0:T(8,128)(2,1)S(1)}, bf16[64,3072]{1,0:T(8,128)(2,1)S(1)}, u32[]{:S(2)}, u32[]{:S(2)}) collective-permute-start(bf16[64,3072]{1,0:T(8,128)(2,1)S(1)} %pad_maximum_fusion.5), channel_id=1, source_target_pairs={{0,8},{1,9},{2,10},{3,11},{4,5},{5,6},{6,7},{7,4},{8,16},{9,17},{1... | collective-permute-start | bytes 1179656 | tf_op jit(solution)/shard_map/ppermute | solution.py:38
  39.5 1.9 %fusion.42 = f32[128,256]{1,0:T(8,128)S(1)} fusion(bf16[1,6144,256]{2,1,0:T(8,128)(2,1)} %param.11, s32[]{:T(128)S(6)} %select_n.61, bf16[32,3072]{1,0:T(8,128)(2,1)S(1)} %collective-permute-done.3, bf16[32,3072]{1,0:T(8,128)(2,1)S(1)} %collective-permute-done.2, bf16[32,3072]{1,0:T(8,128)(2,1)S(1)} %collective-permute-done.1, ...), kind=kOutput, calls=%fused_computation.52 | convolution fusion | flops 204472320 | bytes 2490372 | tf_op jit(solution)/shard_map/dot_general | solution.py:109
  42.2 6.7 %collective-permute-done.4 = bf16[64,3072]{1,0:T(8,128)(2,1)S(1)} collective-permute-done((bf16[64,3072]{1,0:T(8,128)(2,1)S(1)}, bf16[64,3072]{1,0:T(8,128)(2,1)S(1)}, u32[]{:S(2)}, u32[]{:S(2)}) %collective-permute-start.4) | collective-permute-done | bytes 393248 | tf_op jit(solution)/shard_map/ppermute | solution.py:38
  49.4 1.4 %copy-done.2 = bf16[1,6144,256]{2,1,0:T(8,128)(2,1)S(1)} copy-done((bf16[1,6144,256]{2,1,0:T(8,128)(2,1)S(1)}, bf16[1,6144,256]{2,1,0:T(8,128)(2,1)}, u32[]{:S(2)}) %copy-start.2) | copy-done | bytes 3145752
  51.6 2.9 %collective-permute-start.8 = (bf16[64,3072]{1,0:T(8,128)(2,1)S(1)}, bf16[64,3072]{1,0:T(8,128)(2,1)S(1)}, u32[]{:S(2)}, u32[]{:S(2)}) collective-permute-start(bf16[64,3072]{1,0:T(8,128)(2,1)S(1)} %collective-permute-done.6), channel_id=1, source_target_pairs={{0,8},{1,9},{2,10},{3,11},{4,5},{5,6},{6,7},{7,4},{8,16},{9,17},{1... | collective-permute-start | bytes 1179656 | tf_op jit(solution)/shard_map/ppermute | solution.py:38
  56.0 3.8 %collective-permute-done.8 = bf16[64,3072]{1,0:T(8,128)(2,1)S(1)} collective-permute-done((bf16[64,3072]{1,0:T(8,128)(2,1)S(1)}, bf16[64,3072]{1,0:T(8,128)(2,1)S(1)}, u32[]{:S(2)}, u32[]{:S(2)}) %collective-permute-start.8) | collective-permute-done | bytes 393248 | tf_op jit(solution)/shard_map/ppermute | solution.py:38
  68.7 3.4 %collective-permute-start.17 = (bf16[64,3072]{1,0:T(8,128)(2,1)S(1)}, bf16[64,3072]{1,0:T(8,128)(2,1)S(1)}, u32[]{:S(2)}, u32[]{:S(2)}) collective-permute-start(bf16[64,3072]{1,0:T(8,128)(2,1)S(1)} %get-tuple-element.7), channel_id=1, source_target_pairs={{0,8},{1,9},{2,10},{3,11},{4,5},{5,6},{6,7},{7,4},{8,16},{9,17},{1... | collective-permute-start | bytes 1179656 | tf_op jit(solution)/shard_map/ppermute | solution.py:38
  72.5 3.3 %collective-permute-start.22 = (bf16[64,3072]{1,0:T(8,128)(2,1)S(1)}, bf16[64,3072]{1,0:T(8,128)(2,1)S(1)}, u32[]{:S(2)}, u32[]{:S(2)}) collective-permute-start(bf16[64,3072]{1,0:T(8,128)(2,1)S(1)} %slice.197), channel_id=1, source_target_pairs={{0,8},{1,9},{2,10},{3,11},{4,5},{5,6},{6,7},{7,4},{8,16},{9,17},{1... | collective-permute-start | bytes 1179656 | tf_op jit(solution)/shard_map/ppermute | solution.py:38
  77.5 4.0 %collective-permute-start.18 = (bf16[64,3072]{1,0:T(8,128)(2,1)S(1)}, bf16[64,3072]{1,0:T(8,128)(2,1)S(1)}, u32[]{:S(2)}, u32[]{:S(2)}) collective-permute-start(bf16[64,3072]{1,0:T(8,128)(2,1)S(1)} %fusion.80), channel_id=1, source_target_pairs={{0,8},{1,9},{2,10},{3,11},{4,5},{5,6},{6,7},{7,4},{8,16},{9,17},{1... | collective-permute-start | bytes 1179656 | tf_op jit(solution)/shard_map/ppermute | solution.py:38
  82.1 3.3 %collective-permute-done.20 = bf16[64,3072]{1,0:T(8,128)(2,1)S(1)} collective-permute-done((bf16[64,3072]{1,0:T(8,128)(2,1)S(1)}, bf16[64,3072]{1,0:T(8,128)(2,1)S(1)}, u32[]{:S(2)}, u32[]{:S(2)}) %collective-permute-start.20) | collective-permute-done | bytes 393248 | tf_op jit(solution)/shard_map/ppermute | solution.py:38
  85.4 1.4 %collective-permute-done.18 = bf16[64,3072]{1,0:T(8,128)(2,1)S(1)} collective-permute-done((bf16[64,3072]{1,0:T(8,128)(2,1)S(1)}, bf16[64,3072]{1,0:T(8,128)(2,1)S(1)}, u32[]{:S(2)}, u32[]{:S(2)}) %collective-permute-start.18) | collective-permute-done | bytes 393248 | tf_op jit(solution)/shard_map/ppermute | solution.py:38
  86.8 3.9 %collective-permute-done.24 = bf16[64,3072]{1,0:T(8,128)(2,1)S(1)} collective-permute-done((bf16[64,3072]{1,0:T(8,128)(2,1)S(1)}, bf16[64,3072]{1,0:T(8,128)(2,1)S(1)}, u32[]{:S(2)}, u32[]{:S(2)}) %collective-permute-start.24) | collective-permute-done | bytes 393248 | tf_op jit(solution)/shard_map/ppermute | solution.py:38
  91.3 3.0 %collective-permute-start.25 = (bf16[32,3072]{1,0:T(8,128)(2,1)S(1)}, bf16[32,3072]{1,0:T(8,128)(2,1)S(1)}, u32[]{:S(2)}, u32[]{:S(2)}) collective-permute-start(bf16[32,3072]{1,0:T(8,128)(2,1)S(1)} %get-tuple-element.12), channel_id=1, source_target_pairs={{0,3},{1,0},{2,1},{3,2},{4,28},{5,29},{6,30},{7,31},{8,11},{9,8},{... | collective-permute-start | bytes 589832 | tf_op jit(solution)/shard_map/ppermute | solution.py:38
  94.6 3.4 %collective-permute-done.21 = bf16[32,3072]{1,0:T(8,128)(2,1)S(1)} collective-permute-done((bf16[32,3072]{1,0:T(8,128)(2,1)S(1)}, bf16[32,3072]{1,0:T(8,128)(2,1)S(1)}, u32[]{:S(2)}, u32[]{:S(2)}) %collective-permute-start.21) | collective-permute-done | bytes 196640 | tf_op jit(solution)/shard_map/ppermute | solution.py:38
  98.0 1.7 %collective-permute-done.25 = bf16[32,3072]{1,0:T(8,128)(2,1)S(1)} collective-permute-done((bf16[32,3072]{1,0:T(8,128)(2,1)S(1)}, bf16[32,3072]{1,0:T(8,128)(2,1)S(1)}, u32[]{:S(2)}, u32[]{:S(2)}) %collective-permute-start.25) | collective-permute-done | bytes 196640 | tf_op jit(solution)/shard_map/ppermute | solution.py:38
  99.6 1.9 %collective-permute-done.26 = bf16[32,3072]{1,0:T(8,128)(2,1)S(1)} collective-permute-done((bf16[32,3072]{1,0:T(8,128)(2,1)S(1)}, bf16[32,3072]{1,0:T(8,128)(2,1)S(1)}, u32[]{:S(2)}, u32[]{:S(2)}) %collective-permute-start.26) | collective-permute-done | bytes 196640 | tf_op jit(solution)/shard_map/ppermute | solution.py:38
  104.1 3.4 %all-to-all-start.1 = ((bf16[8,2,6144]{2,1,0:T(2,128)(2,1)}), bf16[8,2,6144]{2,1,0:T(2,128)(2,1)S(1)}, u32[]{:S(2)}, u32[]{:S(2)}) async-start(bf16[8,2,6144]{2,1,0:T(2,128)(2,1)} %broadcast_select_fusion), calls=%async_computation.1 | async-start | bytes 393216 | tf_op jit(solution)/shard_map/all_to_all | solution.py:164
  107.6 10.8 %all-to-all-done.1 = bf16[8,2,6144]{2,1,0:T(2,128)(2,1)S(1)} async-done(((bf16[8,2,6144]{2,1,0:T(2,128)(2,1)}), bf16[8,2,6144]{2,1,0:T(2,128)(2,1)S(1)}, u32[]{:S(2)}, u32[]{:S(2)}) %all-to-all-start.1) | async-done | bytes 196640 | tf_op jit(solution)/shard_map/all_to_all | solution.py:164
  (122 shorter events, 28.3 us)
Async XLA Ops:
  4.3 18.9 %all-to-all-start = ((bf16[8,2,6144]{2,1,0:T(2,128)(2,1)}), bf16[8,2,6144]{2,1,0:T(2,128)(2,1)S(1)}, u32[]{:S(2)}, u32[]{:S(2)}) async-start(bf16[8,2,6144]{2,1,0:T(2,128)(2,1)} %reshape.141), calls=%async_computation | async-start | bytes 393216 | tf_op jit(solution)/shard_map/all_to_all | solution.py:67
  24.8 7.0 %collective-permute-start.2 = (bf16[32,3072]{1,0:T(8,128)(2,1)S(1)}, bf16[32,3072]{1,0:T(8,128)(2,1)S(1)}, u32[]{:S(2)}, u32[]{:S(2)}) collective-permute-start(bf16[32,3072]{1,0:T(8,128)(2,1)S(1)} %maximum_select_fusion), channel_id=1, source_target_pairs={{0,1},{1,2},{2,3},{3,0},{4,12},{5,13},{6,14},{7,15},{8,9},{9,10},{... | collective-permute-start | bytes 589832 | tf_op jit(solution)/shard_map/ppermute | solution.py:38
  26.5 8.7 %collective-permute-start.3 = (bf16[32,3072]{1,0:T(8,128)(2,1)S(1)}, bf16[32,3072]{1,0:T(8,128)(2,1)S(1)}, u32[]{:S(2)}, u32[]{:S(2)}) collective-permute-start(bf16[32,3072]{1,0:T(8,128)(2,1)S(1)} %maximum_select_fusion), channel_id=1, source_target_pairs={{0,2},{1,3},{2,0},{3,1},{4,20},{5,21},{6,22},{7,23},{8,10},{9,11},... | collective-permute-start | bytes 589832 | tf_op jit(solution)/shard_map/ppermute | solution.py:38
  29.4 7.9 %collective-permute-start.1 = (bf16[32,3072]{1,0:T(8,128)(2,1)S(1)}, bf16[32,3072]{1,0:T(8,128)(2,1)S(1)}, u32[]{:S(2)}, u32[]{:S(2)}) collective-permute-start(bf16[32,3072]{1,0:T(8,128)(2,1)S(1)} %maximum_select_fusion), channel_id=1, source_target_pairs={{0,3},{1,0},{2,1},{3,2},{4,28},{5,29},{6,30},{7,31},{8,11},{9,8},{... | collective-permute-start | bytes 589832 | tf_op jit(solution)/shard_map/ppermute | solution.py:38
  35.1 19.4 %collective-permute-start.7 = (bf16[64,3072]{1,0:T(8,128)(2,1)S(1)}, bf16[64,3072]{1,0:T(8,128)(2,1)S(1)}, u32[]{:S(2)}, u32[]{:S(2)}) collective-permute-start(bf16[64,3072]{1,0:T(8,128)(2,1)S(1)} %constant_dynamic-update-slice_fusion), channel_id=1, source_target_pairs={{0,8},{1,9},{2,10},{3,11},{4,5},{5,6},{6,7},{7,4},{8,16},{9,17},{1... | collective-permute-start | bytes 1179656 | tf_op jit(solution)/shard_map/ppermute | solution.py:38
  35.7 13.2 %collective-permute-start.5 = (bf16[64,3072]{1,0:T(8,128)(2,1)S(1)}, bf16[64,3072]{1,0:T(8,128)(2,1)S(1)}, u32[]{:S(2)}, u32[]{:S(2)}) collective-permute-start(bf16[64,3072]{1,0:T(8,128)(2,1)S(1)} %constant_dynamic-update-slice_fusion), channel_id=1, source_target_pairs={{0,24},{1,25},{2,26},{3,27},{4,7},{5,4},{6,5},{7,6},{8,0},{9,1},{1... | collective-permute-start | bytes 1179656 | tf_op jit(solution)/shard_map/ppermute | solution.py:38
  37.3 14.3 %collective-permute-start.6 = (bf16[64,3072]{1,0:T(8,128)(2,1)S(1)}, bf16[64,3072]{1,0:T(8,128)(2,1)S(1)}, u32[]{:S(2)}, u32[]{:S(2)}) collective-permute-start(bf16[64,3072]{1,0:T(8,128)(2,1)S(1)} %pad_maximum_fusion.5), channel_id=1, source_target_pairs={{0,8},{1,9},{2,10},{3,11},{4,5},{5,6},{6,7},{7,4},{8,16},{9,17},{1... | collective-permute-start | bytes 1179656 | tf_op jit(solution)/shard_map/ppermute | solution.py:38
  39.0 9.9 %collective-permute-start.4 = (bf16[64,3072]{1,0:T(8,128)(2,1)S(1)}, bf16[64,3072]{1,0:T(8,128)(2,1)S(1)}, u32[]{:S(2)}, u32[]{:S(2)}) collective-permute-start(bf16[64,3072]{1,0:T(8,128)(2,1)S(1)} %pad_maximum_fusion.5), channel_id=1, source_target_pairs={{0,24},{1,25},{2,26},{3,27},{4,7},{5,4},{6,5},{7,6},{8,0},{9,1},{1... | collective-permute-start | bytes 1179656 | tf_op jit(solution)/shard_map/ppermute | solution.py:38
  39.4 21.9 %collective-permute-start.10 = (bf16[128,3072]{1,0:T(8,128)(2,1)S(1)}, bf16[128,3072]{1,0:T(8,128)(2,1)S(1)}, u32[]{:S(2)}, u32[]{:S(2)}) collective-permute-start(bf16[128,3072]{1,0:T(8,128)(2,1)S(1)} %pad_maximum_fusion), channel_id=1, source_target_pairs={{0,4},{1,5},{2,6},{3,7},{4,0},{5,1},{6,2},{7,3},{8,12},{9,13},{10,... | collective-permute-start | bytes 2359304 | tf_op jit(solution)/shard_map/ppermute | solution.py:38
  51.2 9.1 %collective-permute-start.9 = (bf16[64,3072]{1,0:T(8,128)(2,1)S(1)}, bf16[64,3072]{1,0:T(8,128)(2,1)S(1)}, u32[]{:S(2)}, u32[]{:S(2)}) collective-permute-start(bf16[64,3072]{1,0:T(8,128)(2,1)S(1)} %collective-permute-done.5), channel_id=1, source_target_pairs={{0,24},{1,25},{2,26},{3,27},{4,7},{5,4},{6,5},{7,6},{8,0},{9,1},{1... | collective-permute-start | bytes 1179656 | tf_op jit(solution)/shard_map/ppermute | solution.py:38
  51.6 8.2 %collective-permute-start.8 = (bf16[64,3072]{1,0:T(8,128)(2,1)S(1)}, bf16[64,3072]{1,0:T(8,128)(2,1)S(1)}, u32[]{:S(2)}, u32[]{:S(2)}) collective-permute-start(bf16[64,3072]{1,0:T(8,128)(2,1)S(1)} %collective-permute-done.6), channel_id=1, source_target_pairs={{0,8},{1,9},{2,10},{3,11},{4,5},{5,6},{6,7},{7,4},{8,16},{9,17},{1... | collective-permute-start | bytes 1179656 | tf_op jit(solution)/shard_map/ppermute | solution.py:38
  55.5 7.5 %collective-permute-start.11 = (bf16[128,3072]{1,0:T(8,128)(2,1)S(1)}, bf16[128,3072]{1,0:T(8,128)(2,1)S(1)}, u32[]{:S(2)}, u32[]{:S(2)}) collective-permute-start(bf16[128,3072]{1,0:T(8,128)(2,1)S(1)} %constant_dynamic-update-slice_fusion.2), channel_id=1, source_target_pairs={{0,4},{1,5},{2,6},{3,7},{4,0},{5,1},{6,2},{7,3},{8,12},{9,13},{10,... | collective-permute-start | bytes 2359304 | tf_op jit(solution)/shard_map/ppermute | solution.py:38
  66.6 15.0 %collective-permute-start.14 = (bf16[128,3072]{1,0:T(8,128)(2,1)S(1)}, bf16[128,3072]{1,0:T(8,128)(2,1)S(1)}, u32[]{:S(2)}, u32[]{:S(2)}) collective-permute-start(bf16[128,3072]{1,0:T(8,128)(2,1)S(1)} %convolution_convert_fusion.7), channel_id=1, source_target_pairs={{0,4},{1,5},{2,6},{3,7},{4,0},{5,1},{6,2},{7,3},{8,12},{9,13},{10,... | collective-permute-start | bytes 2359304 | tf_op jit(solution)/shard_map/ppermute | solution.py:38
  68.1 7.7 %collective-permute-start.19 = (bf16[128,3072]{1,0:T(8,128)(2,1)S(1)}, bf16[128,3072]{1,0:T(8,128)(2,1)S(1)}, u32[]{:S(2)}, u32[]{:S(2)}) collective-permute-start(bf16[128,3072]{1,0:T(8,128)(2,1)S(1)} %convolution_convert_fusion.1), channel_id=1, source_target_pairs={{0,4},{1,5},{2,6},{3,7},{4,0},{5,1},{6,2},{7,3},{8,12},{9,13},{10,... | collective-permute-start | bytes 2359304 | tf_op jit(solution)/shard_map/ppermute | solution.py:38
  68.7 8.7 %collective-permute-start.17 = (bf16[64,3072]{1,0:T(8,128)(2,1)S(1)}, bf16[64,3072]{1,0:T(8,128)(2,1)S(1)}, u32[]{:S(2)}, u32[]{:S(2)}) collective-permute-start(bf16[64,3072]{1,0:T(8,128)(2,1)S(1)} %get-tuple-element.7), channel_id=1, source_target_pairs={{0,8},{1,9},{2,10},{3,11},{4,5},{5,6},{6,7},{7,4},{8,16},{9,17},{1... | collective-permute-start | bytes 1179656 | tf_op jit(solution)/shard_map/ppermute | solution.py:38
  72.1 9.4 %collective-permute-start.23 = (bf16[64,3072]{1,0:T(8,128)(2,1)S(1)}, bf16[64,3072]{1,0:T(8,128)(2,1)S(1)}, u32[]{:S(2)}, u32[]{:S(2)}) collective-permute-start(bf16[64,3072]{1,0:T(8,128)(2,1)S(1)} %get-tuple-element.8), channel_id=1, source_target_pairs={{0,24},{1,25},{2,26},{3,27},{4,7},{5,4},{6,5},{7,6},{8,0},{9,1},{1... | collective-permute-start | bytes 1179656 | tf_op jit(solution)/shard_map/ppermute | solution.py:38
  72.5 9.5 %collective-permute-start.22 = (bf16[64,3072]{1,0:T(8,128)(2,1)S(1)}, bf16[64,3072]{1,0:T(8,128)(2,1)S(1)}, u32[]{:S(2)}, u32[]{:S(2)}) collective-permute-start(bf16[64,3072]{1,0:T(8,128)(2,1)S(1)} %slice.197), channel_id=1, source_target_pairs={{0,8},{1,9},{2,10},{3,11},{4,5},{5,6},{6,7},{7,4},{8,16},{9,17},{1... | collective-permute-start | bytes 1179656 | tf_op jit(solution)/shard_map/ppermute | solution.py:38
  76.3 9.1 %collective-permute-start.20 = (bf16[64,3072]{1,0:T(8,128)(2,1)S(1)}, bf16[64,3072]{1,0:T(8,128)(2,1)S(1)}, u32[]{:S(2)}, u32[]{:S(2)}) collective-permute-start(bf16[64,3072]{1,0:T(8,128)(2,1)S(1)} %slice.198), channel_id=1, source_target_pairs={{0,24},{1,25},{2,26},{3,27},{4,7},{5,4},{6,5},{7,6},{8,0},{9,1},{1... | collective-permute-start | bytes 1179656 | tf_op jit(solution)/shard_map/ppermute | solution.py:38
  77.5 9.3 %collective-permute-start.18 = (bf16[64,3072]{1,0:T(8,128)(2,1)S(1)}, bf16[64,3072]{1,0:T(8,128)(2,1)S(1)}, u32[]{:S(2)}, u32[]{:S(2)}) collective-permute-start(bf16[64,3072]{1,0:T(8,128)(2,1)S(1)} %fusion.80), channel_id=1, source_target_pairs={{0,8},{1,9},{2,10},{3,11},{4,5},{5,6},{6,7},{7,4},{8,16},{9,17},{1... | collective-permute-start | bytes 1179656 | tf_op jit(solution)/shard_map/ppermute | solution.py:38
  81.6 9.1 %collective-permute-start.24 = (bf16[64,3072]{1,0:T(8,128)(2,1)S(1)}, bf16[64,3072]{1,0:T(8,128)(2,1)S(1)}, u32[]{:S(2)}, u32[]{:S(2)}) collective-permute-start(bf16[64,3072]{1,0:T(8,128)(2,1)S(1)} %fusion.77), channel_id=1, source_target_pairs={{0,24},{1,25},{2,26},{3,27},{4,7},{5,4},{6,5},{7,6},{8,0},{9,1},{1... | collective-permute-start | bytes 1179656 | tf_op jit(solution)/shard_map/ppermute | solution.py:38
  91.0 7.0 %collective-permute-start.21 = (bf16[32,3072]{1,0:T(8,128)(2,1)S(1)}, bf16[32,3072]{1,0:T(8,128)(2,1)S(1)}, u32[]{:S(2)}, u32[]{:S(2)}) collective-permute-start(bf16[32,3072]{1,0:T(8,128)(2,1)S(1)} %slice.149), channel_id=1, source_target_pairs={{0,1},{1,2},{2,3},{3,0},{4,12},{5,13},{6,14},{7,15},{8,9},{9,10},{... | collective-permute-start | bytes 589832 | tf_op jit(solution)/shard_map/ppermute | solution.py:38
  91.3 8.3 %collective-permute-start.25 = (bf16[32,3072]{1,0:T(8,128)(2,1)S(1)}, bf16[32,3072]{1,0:T(8,128)(2,1)S(1)}, u32[]{:S(2)}, u32[]{:S(2)}) collective-permute-start(bf16[32,3072]{1,0:T(8,128)(2,1)S(1)} %get-tuple-element.12), channel_id=1, source_target_pairs={{0,3},{1,0},{2,1},{3,2},{4,28},{5,29},{6,30},{7,31},{8,11},{9,8},{... | collective-permute-start | bytes 589832 | tf_op jit(solution)/shard_map/ppermute | solution.py:38
  94.3 7.2 %collective-permute-start.26 = (bf16[32,3072]{1,0:T(8,128)(2,1)S(1)}, bf16[32,3072]{1,0:T(8,128)(2,1)S(1)}, u32[]{:S(2)}, u32[]{:S(2)}) collective-permute-start(bf16[32,3072]{1,0:T(8,128)(2,1)S(1)} %get-tuple-element.13), channel_id=1, source_target_pairs={{0,2},{1,3},{2,0},{3,1},{4,20},{5,21},{6,22},{7,23},{8,10},{9,11},... | collective-permute-start | bytes 589832 | tf_op jit(solution)/shard_map/ppermute | solution.py:38
  104.1 14.4 %all-to-all-start.1 = ((bf16[8,2,6144]{2,1,0:T(2,128)(2,1)}), bf16[8,2,6144]{2,1,0:T(2,128)(2,1)S(1)}, u32[]{:S(2)}, u32[]{:S(2)}) async-start(bf16[8,2,6144]{2,1,0:T(2,128)(2,1)} %broadcast_select_fusion), calls=%async_computation.1 | async-start | bytes 393216 | tf_op jit(solution)/shard_map/all_to_all | solution.py:164
  (10 other events, 106.2 us)
where the time goes:
time: 120 us; the launch traced here: 119 us
  waiting for transfers between devices  55.7 us (46%)
  starting transfers between devices  42.2 us (35%)
  matrix products  11.8 us (10%)
  other arithmetic  4.66 us (4%)
  local copies, waits for them, and re-layouts  4.36 us (4%)
    ppermute x28, waiting for transfers between devices, move(): return lax.ppermute(value, PLANE, plane_pairs(n_tp, n_dp, step))  34.4 us
    ppermute x28, starting transfers between devices, move(): return lax.ppermute(value, PLANE, plane_pairs(n_tp, n_dp, step))  30.3 us
    all_to_all x1, waiting for transfers between devices, layer(): lax.all_to_all(outgoing, 'expert', split_axis=0, concat_axis=0, tiled=True)  10.8 us
    all_to_all x1, waiting for transfers between devices, layer(): lax.all_to_all(bucket.reshape(groups, MOST, width), 'expert', split_axis=...  10.5 us
    all_to_all x1, starting transfers between devices, layer(): lax.all_to_all(bucket.reshape(groups, MOST, width), 'expert', split_axis=...  8.46 us
    dot_general x16, matrix products, product(): return jnp.dot(block, part, preferred_element_type=jnp.float32)  7.67 us
    all_to_all x1, starting transfers between devices, layer(): lax.all_to_all(outgoing, 'expert', split_axis=0, concat_axis=0, tiled=True)  3.39 us
    unnamed x13, local copies, waits for them, and re-layouts  2.63 us
  transfers between devices with their start and end apart: 30, of which 16 were waited for; matrix products, arithmetic and copies ran while one was open for 9% of the time, Pallas kernels for 0%

commit v1 on v0

--- a/solution.py
+++ b/solution.py
@@ -75,18 +75,28 @@
     pair = jnp.where(
         low, jnp.concatenate([mine, theirs], axis=0), jnp.concatenate([theirs, mine], axis=0)
     )
-    line = jnp.concatenate(
-        [pair, move(pair, first_ring(-1)), move(pair, first_ring(1)), move(pair, first_ring(2))],
-        axis=0,
-    )
+
+    def stacked(*parts):
+        total = jnp.zeros((sum(part.shape[0] for part in parts), half), jnp.bfloat16)
+        at = 0
+        for part in parts:
+            total = lax.dynamic_update_slice(total, part, (at, 0))
+            at += part.shape[0]
+        return total
+
+    in_after = move(pair, first_ring(-1))
+    in_before = move(pair, first_ring(1))
+    in_far = move(pair, first_ring(2))
+    top, bottom = stacked(pair, in_after), stacked(in_before, in_far)
+    line = lax.optimization_barrier(stacked(pair, in_after, in_before, in_far))
     line_rows = line.shape[0]
     cut = line_rows // 2
     ahead, back = second_ring(1), second_ring(-1)
 
-    before_top = move(line[:cut], ahead)
-    after_bottom = move(line[cut:], back)
-    after_top = move(line[:cut], back)
-    before_bottom = move(line[cut:], ahead)
+    before_top = move(top, ahead)
+    after_bottom = move(bottom, back)
+    after_top = move(top, back)
+    before_bottom = move(bottom, ahead)
     far_top = move(before_top, ahead)
     far_bottom = move(after_bottom, back)
     own_x = [
@@ -97,25 +107,43 @@
     ]
     other_x = [swap(block) for block in own_x]
 
-    def reordered(value):
-        blocks = value.reshape(4, 4, 2 * rows, value.shape[-1])
-        return jnp.swapaxes(blocks, 0, 1).reshape(value.shape)
-
-    def both_halves(matrix):
+    seat = 2 * rows
+
+    def both_halves(matrix, kind):
         own = lax.dynamic_slice_in_dim(matrix, core * half, half, 0)
         other = lax.dynamic_slice_in_dim(matrix, (1 - core) * half, half, 0)
 
         def product(block, part):
-            return jnp.dot(block, part, preferred_element_type=jnp.float32)
-
-        own = [product(own_x[i], own) for i in range(4)]
+            return lax.optimization_barrier(
+                jnp.dot(block, part, preferred_element_type=jnp.float32)
+            )
+
+        own = [
+            product(own_x[0], own),
+            product(own_x[1], own),
+            jnp.concatenate(
+                [product(before_top, own), product(before_bottom, own)],
+                axis=0,
+            )
+            if kind == "g"
+            else product(own_x[2], own),
+            product(own_x[3], own),
+        ]
         other = [product(other_x[i], other) for i in range(4)]
-        return jnp.concatenate(own, axis=0) + reordered(jnp.concatenate(other, axis=0))
-
-    gate_val, up_val = both_halves(w_gate[0]), both_halves(w_up[0])
-    activations = (jax.nn.silu(gate_val) * up_val).astype(jnp.bfloat16)
-    for_partner = reordered(activations).reshape(4, line_rows, -1)
-    activations = activations.reshape(4, line_rows, -1)
+        return [
+            own[i]
+            + jnp.concatenate([part[i * seat : (i + 1) * seat] for part in other], axis=0)
+            for i in range(4)
+        ]
+
+    gate_val, up_val = both_halves(w_gate[0], "g"), both_halves(w_up[0], "u")
+    activations = [
+        (jax.nn.silu(gate) * up).astype(jnp.bfloat16) for gate, up in zip(gate_val, up_val)
+    ]
+    for_partner = [
+        jnp.concatenate([part[i * seat : (i + 1) * seat] for part in activations], axis=0)
+        for i in range(4)
+    ]
     down_own = lax.dynamic_slice_in_dim(w_down[0], core * half, half, 1)
     down_other = lax.dynamic_slice_in_dim(w_down[0], (1 - core) * half, half, 1)
 

time: 120 us -> 119 us (level)
  the two profiles are of different devices: /device:TPU:6 before, /device:TPU:1 now
where the time goes in v1:
time: 119 us; the launch traced here: 118 us
  starting transfers between devices  52.7 us (44%)
  waiting for transfers between devices  45 us (38%)
  matrix products  12 us (10%)
  other arithmetic  4.23 us (4%)
  local copies, waits for them, and re-layouts  3.66 us (3%)
    ppermute x28, starting transfers between devices, move(): return lax.ppermute(value, PLANE, plane_pairs(n_tp, n_dp, step))  40.3 us
    ppermute x28, waiting for transfers between devices, move(): return lax.ppermute(value, PLANE, plane_pairs(n_tp, n_dp, step))  26.1 us
    all_to_all x1, waiting for transfers between devices, layer(): lax.all_to_all(outgoing, 'expert', split_axis=0, concat_axis=0, tiled=True)  9.87 us
    all_to_all x1, starting transfers between devices, layer(): lax.all_to_all(bucket.reshape(groups, MOST, width), 'expert', split_axis=...  9 us
    all_to_all x1, waiting for transfers between devices, layer(): lax.all_to_all(bucket.reshape(groups, MOST, width), 'expert', split_axis=...  8.99 us
    dot_general x17, matrix products, product(): jnp.dot(block, part, preferred_element_type=jnp.float32)  7.89 us
    all_to_all x1, starting transfers between devices, layer(): lax.all_to_all(outgoing, 'expert', split_axis=0, concat_axis=0, tiled=True)  3.39 us
  transfers between devices with their start and end apart: 30, of which 16 were waited for; matrix products, arithmetic and copies ran while one was open for 9% of the time, Pallas kernels for 0%

profile of v1, /device:TPU:1, one launch (start us, length us, event | category | flops | bytes accessed | tf_op | source)
XLA Modules:
  0.0 118.2 jit_solution(5444219920106479580)
XLA Ops:
  4.3 9.0 %all-to-all-start = ((bf16[8,2,6144]{2,1,0:T(2,128)(2,1)}), bf16[8,2,6144]{2,1,0:T(2,128)(2,1)S(1)}, u32[]{:S(2)}, u32[]{:S(2)}) async-start(bf16[8,2,6144]{2,1,0:T(2,128)(2,1)} %reshape.109), calls=%async_computation | async-start | bytes 393216 | tf_op jit(solution)/shard_map/all_to_all | solution.py:67
  13.3 9.0 %all-to-all-done = bf16[8,2,6144]{2,1,0:T(2,128)(2,1)S(1)} async-done(((bf16[8,2,6144]{2,1,0:T(2,128)(2,1)}), bf16[8,2,6144]{2,1,0:T(2,128)(2,1)S(1)}, u32[]{:S(2)}, u32[]{:S(2)}) %all-to-all-start) | async-done | bytes 196640 | tf_op jit(solution)/shard_map/all_to_all | solution.py:67
  22.4 2.5 %collective-permute-start = (bf16[16,3072]{1,0:T(8,128)(2,1)S(1)}, bf16[16,3072]{1,0:T(8,128)(2,1)S(1)}, u32[]{:S(2)}, u32[]{:S(2)}) collective-permute-start(bf16[16,3072]{1,0:T(8,128)(2,1)S(1)} %get-tuple-element.18), channel_id=1, source_target_pairs={{0,4},{1,5},{2,6},{3,7},{4,0},{5,1},{6,2},{7,3},{8,12},{9,13},{10,... | collective-permute-start | bytes 294920 | tf_op jit(solution)/shard_map/ppermute | solution.py:38
  25.9 2.6 %collective-permute-start.1 = (bf16[32,3072]{1,0:T(8,128)(2,1)S(1)}, bf16[32,3072]{1,0:T(8,128)(2,1)S(1)}, u32[]{:S(2)}, u32[]{:S(2)}) collective-permute-start(bf16[32,3072]{1,0:T(8,128)(2,1)S(1)} %maximum_select_fusion), channel_id=1, source_target_pairs={{0,3},{1,0},{2,1},{3,2},{4,28},{5,29},{6,30},{7,31},{8,11},{9,8},{... | collective-permute-start | bytes 589832 | tf_op jit(solution)/shard_map/ppermute | solution.py:38
  29.7 3.5 %collective-permute-done.1 = bf16[32,3072]{1,0:T(8,128)(2,1)S(1)} collective-permute-done((bf16[32,3072]{1,0:T(8,128)(2,1)S(1)}, bf16[32,3072]{1,0:T(8,128)(2,1)S(1)}, u32[]{:S(2)}, u32[]{:S(2)}) %collective-permute-start.1) | collective-permute-done | bytes 196640 | tf_op jit(solution)/shard_map/ppermute | solution.py:38
  37.0 1.8 %collective-permute-start.9 = (bf16[64,3072]{1,0:T(8,128)(2,1)S(1)}, bf16[64,3072]{1,0:T(8,128)(2,1)S(1)}, u32[]{:S(2)}, u32[]{:S(2)}) collective-permute-start(bf16[64,3072]{1,0:T(8,128)(2,1)S(1)} %get-tuple-element.14), channel_id=1, source_target_pairs={{0,8},{1,9},{2,10},{3,11},{4,5},{5,6},{6,7},{7,4},{8,16},{9,17},{1... | collective-permute-start | bytes 1179656 | tf_op jit(solution)/shard_map/ppermute | solution.py:38
  39.8 3.3 %collective-permute-start.4 = (bf16[128,3072]{1,0:T(8,128)(2,1)S(1)}, bf16[128,3072]{1,0:T(8,128)(2,1)S(1)}, u32[]{:S(2)}, u32[]{:S(2)}) collective-permute-start(bf16[128,3072]{1,0:T(8,128)(2,1)S(1)} %get-tuple-element.13), channel_id=1, source_target_pairs={{0,4},{1,5},{2,6},{3,7},{4,0},{5,1},{6,2},{7,3},{8,12},{9,13},{10,... | collective-permute-start | bytes 2359304 | tf_op jit(solution)/shard_map/ppermute | solution.py:38
  43.0 1.8 %fusion.26 = f32[128,256]{1,0:T(8,128)S(1)} fusion(bf16[128,3072]{1,0:T(8,128)(2,1)S(1)} %get-tuple-element.13, bf16[1,6144,256]{2,1,0:T(8,128)(2,1)} %param.12, s32[]{:T(128)S(6)} %select_n.61), kind=kOutput, calls=%fused_computation.36 | convolution fusion | flops 201326592 | bytes 2490372 | tf_op jit(solution)/shard_map/dot_general | solution.py:118
  48.0 3.6 %collective-permute-start.10 = (bf16[128,3072]{1,0:T(8,128)(2,1)S(1)}, bf16[128,3072]{1,0:T(8,128)(2,1)S(1)}, u32[]{:S(2)}, u32[]{:S(2)}) collective-permute-start(bf16[128,3072]{1,0:T(8,128)(2,1)S(1)} %constant_dynamic-update-slice_fusion.4), channel_id=1, source_target_pairs={{0,4},{1,5},{2,6},{3,7},{4,0},{5,1},{6,2},{7,3},{8,12},{9,13},{10,... | collective-permute-start | bytes 2359304 | tf_op jit(solution)/shard_map/ppermute | solution.py:38
  51.7 2.7 %collective-permute-start.12 = (bf16[64,3072]{1,0:T(8,128)(2,1)S(1)}, bf16[64,3072]{1,0:T(8,128)(2,1)S(1)}, u32[]{:S(2)}, u32[]{:S(2)}) collective-permute-start(bf16[64,3072]{1,0:T(8,128)(2,1)S(1)} %collective-permute-done.6), channel_id=1, source_target_pairs={{0,24},{1,25},{2,26},{3,27},{4,7},{5,4},{6,5},{7,6},{8,0},{9,1},{1... | collective-permute-start | bytes 1179656 | tf_op jit(solution)/shard_map/ppermute | solution.py:38
  55.1 4.7 %collective-permute-done.11 = bf16[64,3072]{1,0:T(8,128)(2,1)S(1)} collective-permute-done((bf16[64,3072]{1,0:T(8,128)(2,1)S(1)}, bf16[64,3072]{1,0:T(8,128)(2,1)S(1)}, u32[]{:S(2)}, u32[]{:S(2)}) %collective-permute-start.11) | collective-permute-done | bytes 393248 | tf_op jit(solution)/shard_map/ppermute | solution.py:38
  60.6 1.6 %collective-permute-start.13 = (bf16[128,3072]{1,0:T(8,128)(2,1)S(1)}, bf16[128,3072]{1,0:T(8,128)(2,1)S(1)}, u32[]{:S(2)}, u32[]{:S(2)}) collective-permute-start(bf16[128,3072]{1,0:T(8,128)(2,1)S(1)} %constant_dynamic-update-slice_fusion.6), channel_id=1, source_target_pairs={{0,4},{1,5},{2,6},{3,7},{4,0},{5,1},{6,2},{7,3},{8,12},{9,13},{10,... | collective-permute-start | bytes 2359304 | tf_op jit(solution)/shard_map/ppermute | solution.py:38
  69.3 2.7 %collective-permute-start.23 = (bf16[64,3072]{1,0:T(8,128)(2,1)S(1)}, bf16[64,3072]{1,0:T(8,128)(2,1)S(1)}, u32[]{:S(2)}, u32[]{:S(2)}) collective-permute-start(bf16[64,3072]{1,0:T(8,128)(2,1)S(1)} %get-tuple-element.8), channel_id=1, source_target_pairs={{0,24},{1,25},{2,26},{3,27},{4,7},{5,4},{6,5},{7,6},{8,0},{9,1},{1... | collective-permute-start | bytes 1179656 | tf_op jit(solution)/shard_map/ppermute | solution.py:38
  74.7 2.0 %collective-permute-done.23 = bf16[64,3072]{1,0:T(8,128)(2,1)S(1)} collective-permute-done((bf16[64,3072]{1,0:T(8,128)(2,1)S(1)}, bf16[64,3072]{1,0:T(8,128)(2,1)S(1)}, u32[]{:S(2)}, u32[]{:S(2)}) %collective-permute-start.23) | collective-permute-done | bytes 393248 | tf_op jit(solution)/shard_map/ppermute | solution.py:38
  76.8 3.2 %collective-permute-start.24 = (bf16[64,3072]{1,0:T(8,128)(2,1)S(1)}, bf16[64,3072]{1,0:T(8,128)(2,1)S(1)}, u32[]{:S(2)}, u32[]{:S(2)}) collective-permute-start(bf16[64,3072]{1,0:T(8,128)(2,1)S(1)} %fusion.80), channel_id=1, source_target_pairs={{0,24},{1,25},{2,26},{3,27},{4,7},{5,4},{6,5},{7,6},{8,0},{9,1},{1... | collective-permute-start | bytes 1179656 | tf_op jit(solution)/shard_map/ppermute | solution.py:38
  81.8 3.3 %collective-permute-done.24 = bf16[64,3072]{1,0:T(8,128)(2,1)S(1)} collective-permute-done((bf16[64,3072]{1,0:T(8,128)(2,1)S(1)}, bf16[64,3072]{1,0:T(8,128)(2,1)S(1)}, u32[]{:S(2)}, u32[]{:S(2)}) %collective-permute-start.24) | collective-permute-done | bytes 393248 | tf_op jit(solution)/shard_map/ppermute | solution.py:38
  85.1 3.2 %collective-permute-done.18 = bf16[64,3072]{1,0:T(8,128)(2,1)S(1)} collective-permute-done((bf16[64,3072]{1,0:T(8,128)(2,1)S(1)}, bf16[64,3072]{1,0:T(8,128)(2,1)S(1)}, u32[]{:S(2)}, u32[]{:S(2)}) %collective-permute-start.18) | collective-permute-done | bytes 393248 | tf_op jit(solution)/shard_map/ppermute | solution.py:38
  88.7 2.8 %collective-permute-start.25 = (bf16[32,3072]{1,0:T(8,128)(2,1)S(1)}, bf16[32,3072]{1,0:T(8,128)(2,1)S(1)}, u32[]{:S(2)}, u32[]{:S(2)}) collective-permute-start(bf16[32,3072]{1,0:T(8,128)(2,1)S(1)} %get-tuple-element.9), channel_id=1, source_target_pairs={{0,3},{1,0},{2,1},{3,2},{4,28},{5,29},{6,30},{7,31},{8,11},{9,8},{... | collective-permute-start | bytes 589832 | tf_op jit(solution)/shard_map/ppermute | solution.py:38
  92.6 1.9 %collective-permute-done.21 = bf16[32,3072]{1,0:T(8,128)(2,1)S(1)} collective-permute-done((bf16[32,3072]{1,0:T(8,128)(2,1)S(1)}, bf16[32,3072]{1,0:T(8,128)(2,1)S(1)}, u32[]{:S(2)}, u32[]{:S(2)}) %collective-permute-start.21) | collective-permute-done | bytes 196640 | tf_op jit(solution)/shard_map/ppermute | solution.py:38
  94.5 1.8 %collective-permute-done.25 = bf16[32,3072]{1,0:T(8,128)(2,1)S(1)} collective-permute-done((bf16[32,3072]{1,0:T(8,128)(2,1)S(1)}, bf16[32,3072]{1,0:T(8,128)(2,1)S(1)}, u32[]{:S(2)}, u32[]{:S(2)}) %collective-permute-start.25) | collective-permute-done | bytes 196640 | tf_op jit(solution)/shard_map/ppermute | solution.py:38
  96.2 1.5 %collective-permute-done.26 = bf16[32,3072]{1,0:T(8,128)(2,1)S(1)} collective-permute-done((bf16[32,3072]{1,0:T(8,128)(2,1)S(1)}, bf16[32,3072]{1,0:T(8,128)(2,1)S(1)}, u32[]{:S(2)}, u32[]{:S(2)}) %collective-permute-start.26) | collective-permute-done | bytes 196640 | tf_op jit(solution)/shard_map/ppermute | solution.py:38
  97.9 4.1 %collective-permute-start.27 = (bf16[16,3072]{1,0:T(8,128)(2,1)S(1)}, bf16[16,3072]{1,0:T(8,128)(2,1)S(1)}, u32[]{:S(2)}, u32[]{:S(2)}) collective-permute-start(bf16[16,3072]{1,0:T(8,128)(2,1)S(1)} %get-tuple-element.12), channel_id=1, source_target_pairs={{0,4},{1,5},{2,6},{3,7},{4,0},{5,1},{6,2},{7,3},{8,12},{9,13},{10,... | collective-permute-start | bytes 294920 | tf_op jit(solution)/shard_map/ppermute | solution.py:38
  103.9 3.4 %all-to-all-start.1 = ((bf16[8,2,6144]{2,1,0:T(2,128)(2,1)}), bf16[8,2,6144]{2,1,0:T(2,128)(2,1)S(1)}, u32[]{:S(2)}, u32[]{:S(2)}) async-start(bf16[8,2,6144]{2,1,0:T(2,128)(2,1)} %broadcast_select_fusion), calls=%async_computation.1 | async-start | bytes 393216 | tf_op jit(solution)/shard_map/all_to_all | solution.py:192
  107.4 9.9 %all-to-all-done.1 = bf16[8,2,6144]{2,1,0:T(2,128)(2,1)S(1)} async-done(((bf16[8,2,6144]{2,1,0:T(2,128)(2,1)}), bf16[8,2,6144]{2,1,0:T(2,128)(2,1)S(1)}, u32[]{:S(2)}, u32[]{:S(2)}) %all-to-all-start.1) | async-done | bytes 196640 | tf_op jit(solution)/shard_map/all_to_all | solution.py:192
  (129 shorter events, 32.1 us)
Async XLA Ops:
  4.3 18.0 %all-to-all-start = ((bf16[8,2,6144]{2,1,0:T(2,128)(2,1)}), bf16[8,2,6144]{2,1,0:T(2,128)(2,1)S(1)}, u32[]{:S(2)}, u32[]{:S(2)}) async-start(bf16[8,2,6144]{2,1,0:T(2,128)(2,1)} %reshape.109), calls=%async_computation | async-start | bytes 393216 | tf_op jit(solution)/shard_map/all_to_all | solution.py:67
  25.9 7.3 %collective-permute-start.1 = (bf16[32,3072]{1,0:T(8,128)(2,1)S(1)}, bf16[32,3072]{1,0:T(8,128)(2,1)S(1)}, u32[]{:S(2)}, u32[]{:S(2)}) collective-permute-start(bf16[32,3072]{1,0:T(8,128)(2,1)S(1)} %maximum_select_fusion), channel_id=1, source_target_pairs={{0,3},{1,0},{2,1},{3,2},{4,28},{5,29},{6,30},{7,31},{8,11},{9,8},{... | collective-permute-start | bytes 589832 | tf_op jit(solution)/shard_map/ppermute | solution.py:38
  28.5 8.5 %collective-permute-start.3 = (bf16[32,3072]{1,0:T(8,128)(2,1)S(1)}, bf16[32,3072]{1,0:T(8,128)(2,1)S(1)}, u32[]{:S(2)}, u32[]{:S(2)}) collective-permute-start(bf16[32,3072]{1,0:T(8,128)(2,1)S(1)} %maximum_select_fusion), channel_id=1, source_target_pairs={{0,2},{1,3},{2,0},{3,1},{4,20},{5,21},{6,22},{7,23},{8,10},{9,11},... | collective-permute-start | bytes 589832 | tf_op jit(solution)/shard_map/ppermute | solution.py:38
  29.0 7.9 %collective-permute-start.2 = (bf16[32,3072]{1,0:T(8,128)(2,1)S(1)}, bf16[32,3072]{1,0:T(8,128)(2,1)S(1)}, u32[]{:S(2)}, u32[]{:S(2)}) collective-permute-start(bf16[32,3072]{1,0:T(8,128)(2,1)S(1)} %maximum_select_fusion), channel_id=1, source_target_pairs={{0,1},{1,2},{2,3},{3,0},{4,12},{5,13},{6,14},{7,15},{8,9},{9,10},{... | collective-permute-start | bytes 589832 | tf_op jit(solution)/shard_map/ppermute | solution.py:38
  33.2 14.3 %collective-permute-start.8 = (bf16[64,3072]{1,0:T(8,128)(2,1)S(1)}, bf16[64,3072]{1,0:T(8,128)(2,1)S(1)}, u32[]{:S(2)}, u32[]{:S(2)}) collective-permute-start(bf16[64,3072]{1,0:T(8,128)(2,1)S(1)} %pad_maximum_fusion), channel_id=1, source_target_pairs={{0,8},{1,9},{2,10},{3,11},{4,5},{5,6},{6,7},{7,4},{8,16},{9,17},{1... | collective-permute-start | bytes 1179656 | tf_op jit(solution)/shard_map/ppermute | solution.py:38
  34.6 10.6 %collective-permute-start.5 = (bf16[64,3072]{1,0:T(8,128)(2,1)S(1)}, bf16[64,3072]{1,0:T(8,128)(2,1)S(1)}, u32[]{:S(2)}, u32[]{:S(2)}) collective-permute-start(bf16[64,3072]{1,0:T(8,128)(2,1)S(1)} %pad_maximum_fusion), channel_id=1, source_target_pairs={{0,24},{1,25},{2,26},{3,27},{4,7},{5,4},{6,5},{7,6},{8,0},{9,1},{1... | collective-permute-start | bytes 1179656 | tf_op jit(solution)/shard_map/ppermute | solution.py:38
  37.0 10.5 %collective-permute-start.9 = (bf16[64,3072]{1,0:T(8,128)(2,1)S(1)}, bf16[64,3072]{1,0:T(8,128)(2,1)S(1)}, u32[]{:S(2)}, u32[]{:S(2)}) collective-permute-start(bf16[64,3072]{1,0:T(8,128)(2,1)S(1)} %get-tuple-element.14), channel_id=1, source_target_pairs={{0,8},{1,9},{2,10},{3,11},{4,5},{5,6},{6,7},{7,4},{8,16},{9,17},{1... | collective-permute-start | bytes 1179656 | tf_op jit(solution)/shard_map/ppermute | solution.py:38
  38.8 7.0 %collective-permute-start.6 = (bf16[64,3072]{1,0:T(8,128)(2,1)S(1)}, bf16[64,3072]{1,0:T(8,128)(2,1)S(1)}, u32[]{:S(2)}, u32[]{:S(2)}) collective-permute-start(bf16[64,3072]{1,0:T(8,128)(2,1)S(1)} %get-tuple-element.14), channel_id=1, source_target_pairs={{0,24},{1,25},{2,26},{3,27},{4,7},{5,4},{6,5},{7,6},{8,0},{9,1},{1... | collective-permute-start | bytes 1179656 | tf_op jit(solution)/shard_map/ppermute | solution.py:38
  39.8 22.5 %collective-permute-start.4 = (bf16[128,3072]{1,0:T(8,128)(2,1)S(1)}, bf16[128,3072]{1,0:T(8,128)(2,1)S(1)}, u32[]{:S(2)}, u32[]{:S(2)}) collective-permute-start(bf16[128,3072]{1,0:T(8,128)(2,1)S(1)} %get-tuple-element.13), channel_id=1, source_target_pairs={{0,4},{1,5},{2,6},{3,7},{4,0},{5,1},{6,2},{7,3},{8,12},{9,13},{10,... | collective-permute-start | bytes 2359304 | tf_op jit(solution)/shard_map/ppermute | solution.py:38
  48.0 15.1 %collective-permute-start.10 = (bf16[128,3072]{1,0:T(8,128)(2,1)S(1)}, bf16[128,3072]{1,0:T(8,128)(2,1)S(1)}, u32[]{:S(2)}, u32[]{:S(2)}) collective-permute-start(bf16[128,3072]{1,0:T(8,128)(2,1)S(1)} %constant_dynamic-update-slice_fusion.4), channel_id=1, source_target_pairs={{0,4},{1,5},{2,6},{3,7},{4,0},{5,1},{6,2},{7,3},{8,12},{9,13},{10,... | collective-permute-start | bytes 2359304 | tf_op jit(solution)/shard_map/ppermute | solution.py:38
  51.5 12.3 %collective-permute-start.7 = (bf16[128,3072]{1,0:T(8,128)(2,1)S(1)}, bf16[128,3072]{1,0:T(8,128)(2,1)S(1)}, u32[]{:S(2)}, u32[]{:S(2)}) collective-permute-start(bf16[128,3072]{1,0:T(8,128)(2,1)S(1)} %constant_dynamic-update-slice_fusion.2), channel_id=1, source_target_pairs={{0,4},{1,5},{2,6},{3,7},{4,0},{5,1},{6,2},{7,3},{8,12},{9,13},{10,... | collective-permute-start | bytes 2359304 | tf_op jit(solution)/shard_map/ppermute | solution.py:38
  51.6 8.1 %collective-permute-start.11 = (bf16[64,3072]{1,0:T(8,128)(2,1)S(1)}, bf16[64,3072]{1,0:T(8,128)(2,1)S(1)}, u32[]{:S(2)}, u32[]{:S(2)}) collective-permute-start(bf16[64,3072]{1,0:T(8,128)(2,1)S(1)} %collective-permute-done.8), channel_id=1, source_target_pairs={{0,8},{1,9},{2,10},{3,11},{4,5},{5,6},{6,7},{7,4},{8,16},{9,17},{1... | collective-permute-start | bytes 1179656 | tf_op jit(solution)/shard_map/ppermute | solution.py:38
  51.7 8.2 %collective-permute-start.12 = (bf16[64,3072]{1,0:T(8,128)(2,1)S(1)}, bf16[64,3072]{1,0:T(8,128)(2,1)S(1)}, u32[]{:S(2)}, u32[]{:S(2)}) collective-permute-start(bf16[64,3072]{1,0:T(8,128)(2,1)S(1)} %collective-permute-done.6), channel_id=1, source_target_pairs={{0,24},{1,25},{2,26},{3,27},{4,7},{5,4},{6,5},{7,6},{8,0},{9,1},{1... | collective-permute-start | bytes 1179656 | tf_op jit(solution)/shard_map/ppermute | solution.py:38
  66.7 13.5 %collective-permute-start.14 = (bf16[128,3072]{1,0:T(8,128)(2,1)S(1)}, bf16[128,3072]{1,0:T(8,128)(2,1)S(1)}, u32[]{:S(2)}, u32[]{:S(2)}) collective-permute-start(bf16[128,3072]{1,0:T(8,128)(2,1)S(1)} %convolution_convert_fusion.7), channel_id=1, source_target_pairs={{0,4},{1,5},{2,6},{3,7},{4,0},{5,1},{6,2},{7,3},{8,12},{9,13},{10,... | collective-permute-start | bytes 2359304 | tf_op jit(solution)/shard_map/ppermute | solution.py:38
  69.2 10.8 %collective-permute-start.17 = (bf16[64,3072]{1,0:T(8,128)(2,1)S(1)}, bf16[64,3072]{1,0:T(8,128)(2,1)S(1)}, u32[]{:S(2)}, u32[]{:S(2)}) collective-permute-start(bf16[64,3072]{1,0:T(8,128)(2,1)S(1)} %get-tuple-element.7), channel_id=1, source_target_pairs={{0,8},{1,9},{2,10},{3,11},{4,5},{5,6},{6,7},{7,4},{8,16},{9,17},{1... | collective-permute-start | bytes 1179656 | tf_op jit(solution)/shard_map/ppermute | solution.py:38
  69.3 7.4 %collective-permute-start.23 = (bf16[64,3072]{1,0:T(8,128)(2,1)S(1)}, bf16[64,3072]{1,0:T(8,128)(2,1)S(1)}, u32[]{:S(2)}, u32[]{:S(2)}) collective-permute-start(bf16[64,3072]{1,0:T(8,128)(2,1)S(1)} %get-tuple-element.8), channel_id=1, source_target_pairs={{0,24},{1,25},{2,26},{3,27},{4,7},{5,4},{6,5},{7,6},{8,0},{9,1},{1... | collective-permute-start | bytes 1179656 | tf_op jit(solution)/shard_map/ppermute | solution.py:38
  72.4 8.5 %collective-permute-start.20 = (bf16[64,3072]{1,0:T(8,128)(2,1)S(1)}, bf16[64,3072]{1,0:T(8,128)(2,1)S(1)}, u32[]{:S(2)}, u32[]{:S(2)}) collective-permute-start(bf16[64,3072]{1,0:T(8,128)(2,1)S(1)} %slice.376), channel_id=1, source_target_pairs={{0,24},{1,25},{2,26},{3,27},{4,7},{5,4},{6,5},{7,6},{8,0},{9,1},{1... | collective-permute-start | bytes 1179656 | tf_op jit(solution)/shard_map/ppermute | solution.py:38
  73.4 8.4 %collective-permute-start.22 = (bf16[64,3072]{1,0:T(8,128)(2,1)S(1)}, bf16[64,3072]{1,0:T(8,128)(2,1)S(1)}, u32[]{:S(2)}, u32[]{:S(2)}) collective-permute-start(bf16[64,3072]{1,0:T(8,128)(2,1)S(1)} %slice.375), channel_id=1, source_target_pairs={{0,8},{1,9},{2,10},{3,11},{4,5},{5,6},{6,7},{7,4},{8,16},{9,17},{1... | collective-permute-start | bytes 1179656 | tf_op jit(solution)/shard_map/ppermute | solution.py:38
  76.8 8.3 %collective-permute-start.24 = (bf16[64,3072]{1,0:T(8,128)(2,1)S(1)}, bf16[64,3072]{1,0:T(8,128)(2,1)S(1)}, u32[]{:S(2)}, u32[]{:S(2)}) collective-permute-start(bf16[64,3072]{1,0:T(8,128)(2,1)S(1)} %fusion.80), channel_id=1, source_target_pairs={{0,24},{1,25},{2,26},{3,27},{4,7},{5,4},{6,5},{7,6},{8,0},{9,1},{1... | collective-permute-start | bytes 1179656 | tf_op jit(solution)/shard_map/ppermute | solution.py:38
  80.1 8.2 %collective-permute-start.18 = (bf16[64,3072]{1,0:T(8,128)(2,1)S(1)}, bf16[64,3072]{1,0:T(8,128)(2,1)S(1)}, u32[]{:S(2)}, u32[]{:S(2)}) collective-permute-start(bf16[64,3072]{1,0:T(8,128)(2,1)S(1)} %fusion.83), channel_id=1, source_target_pairs={{0,8},{1,9},{2,10},{3,11},{4,5},{5,6},{6,7},{7,4},{8,16},{9,17},{1... | collective-permute-start | bytes 1179656 | tf_op jit(solution)/shard_map/ppermute | solution.py:38
  88.7 5.8 %collective-permute-start.21 = (bf16[32,3072]{1,0:T(8,128)(2,1)S(1)}, bf16[32,3072]{1,0:T(8,128)(2,1)S(1)}, u32[]{:S(2)}, u32[]{:S(2)}) collective-permute-start(bf16[32,3072]{1,0:T(8,128)(2,1)S(1)} %slice.335), channel_id=1, source_target_pairs={{0,1},{1,2},{2,3},{3,0},{4,12},{5,13},{6,14},{7,15},{8,9},{9,10},{... | collective-permute-start | bytes 589832 | tf_op jit(solution)/shard_map/ppermute | solution.py:38
  88.7 7.5 %collective-permute-start.25 = (bf16[32,3072]{1,0:T(8,128)(2,1)S(1)}, bf16[32,3072]{1,0:T(8,128)(2,1)S(1)}, u32[]{:S(2)}, u32[]{:S(2)}) collective-permute-start(bf16[32,3072]{1,0:T(8,128)(2,1)S(1)} %get-tuple-element.9), channel_id=1, source_target_pairs={{0,3},{1,0},{2,1},{3,2},{4,28},{5,29},{6,30},{7,31},{8,11},{9,8},{... | collective-permute-start | bytes 589832 | tf_op jit(solution)/shard_map/ppermute | solution.py:38
  91.5 6.3 %collective-permute-start.26 = (bf16[32,3072]{1,0:T(8,128)(2,1)S(1)}, bf16[32,3072]{1,0:T(8,128)(2,1)S(1)}, u32[]{:S(2)}, u32[]{:S(2)}) collective-permute-start(bf16[32,3072]{1,0:T(8,128)(2,1)S(1)} %get-tuple-element.10), channel_id=1, source_target_pairs={{0,2},{1,3},{2,0},{3,1},{4,20},{5,21},{6,22},{7,23},{8,10},{9,11},... | collective-permute-start | bytes 589832 | tf_op jit(solution)/shard_map/ppermute | solution.py:38
  103.9 13.4 %all-to-all-start.1 = ((bf16[8,2,6144]{2,1,0:T(2,128)(2,1)}), bf16[8,2,6144]{2,1,0:T(2,128)(2,1)S(1)}, u32[]{:S(2)}, u32[]{:S(2)}) async-start(bf16[8,2,6144]{2,1,0:T(2,128)(2,1)} %broadcast_select_fusion), calls=%async_computation.1 | async-start | bytes 393216 | tf_op jit(solution)/shard_map/all_to_all | solution.py:192
  (10 other events, 118.5 us)

commit v2 on v1

--- a/solution.py
+++ b/solution.py
@@ -186,14 +186,15 @@
     ).astype(jnp.bfloat16)
     mine = jnp.where(low, pair_sum[:rows], pair_sum[rows:])
     theirs = swap(jnp.where(low, pair_sum[rows:], pair_sum[:rows]))
-    summed = joined(mine, theirs)
-
-    outgoing = summed.reshape(groups, MOST, width)
+    outgoing = jnp.concatenate(
+        [mine.reshape(groups, MOST, half), theirs.reshape(groups, MOST, half)], axis=1
+    )
     returned = lax.all_to_all(outgoing, "expert", split_axis=0, concat_axis=0, tiled=True)
-    picked = jnp.dot(
-        selector.T, returned.reshape(groups * MOST, width), preferred_element_type=jnp.float32
-    )
-    picked = picked.reshape(hidden.shape[0], 2, width)
+    parts = [
+        jnp.dot(selector.T, part.reshape(rows, half), preferred_element_type=jnp.float32)
+        for part in (returned[:, :MOST], returned[:, MOST:])
+    ]
+    picked = joined(*parts).reshape(hidden.shape[0], 2, width)
     first = jax.nn.sigmoid(router_logits[:, 0] - router_logits[:, 1])
     second = jax.nn.sigmoid(router_logits[:, 1] - router_logits[:, 0])
     route_weight = jnp.stack([first, second], axis=1)

time: 119 us -> 119 us (level)
  no operation moved by 1% of the time
where the time goes in v2:
time: 119 us
  starting transfers between devices  52.7 us (44%)
  waiting for transfers between devices  44.9 us (38%)
  matrix products  11.6 us (10%)
  other arithmetic  5.11 us (4%)
  local copies, waits for them, and re-layouts  3.94 us (3%)
    ppermute x28, starting transfers between devices, move(): return lax.ppermute(value, PLANE, plane_pairs(n_tp, n_dp, step))  40.3 us
    ppermute x28, waiting for transfers between devices, move(): return lax.ppermute(value, PLANE, plane_pairs(n_tp, n_dp, step))  26.1 us
    all_to_all x1, waiting for transfers between devices, layer(): lax.all_to_all(outgoing, 'expert', split_axis=0, concat_axis=0, tiled=True)  9.79 us
    all_to_all x1, starting transfers between devices, layer(): lax.all_to_all(bucket.reshape(groups, MOST, width), 'expert', split_axis=...  9 us
    all_to_all x1, waiting for transfers between devices, layer(): lax.all_to_all(bucket.reshape(groups, MOST, width), 'expert', split_axis=...  8.99 us
    dot_general x17, matrix products, product(): jnp.dot(block, part, preferred_element_type=jnp.float32)  7.89 us
    all_to_all x1, starting transfers between devices, layer(): lax.all_to_all(outgoing, 'expert', split_axis=0, concat_axis=0, tiled=True)  3.39 us
  transfers between devices with their start and end apart: 30, of which 16 were waited for; matrix products, arithmetic and copies ran while one was open for 9% of the time, Pallas kernels for 0%

profile of v2, /device:TPU:1, one launch (start us, length us, event | category | flops | bytes accessed | tf_op | source)
XLA Modules:
  0.0 118.9 jit_solution(5432764755474145556)
XLA Ops:
  4.3 9.0 %all-to-all-start = ((bf16[8,2,6144]{2,1,0:T(2,128)(2,1)}), bf16[8,2,6144]{2,1,0:T(2,128)(2,1)S(1)}, u32[]{:S(2)}, u32[]{:S(2)}) async-start(bf16[8,2,6144]{2,1,0:T(2,128)(2,1)} %reshape.111), calls=%async_computation | async-start | bytes 393216 | tf_op jit(solution)/shard_map/all_to_all | solution.py:67
  13.3 9.0 %all-to-all-done = bf16[8,2,6144]{2,1,0:T(2,128)(2,1)S(1)} async-done(((bf16[8,2,6144]{2,1,0:T(2,128)(2,1)}), bf16[8,2,6144]{2,1,0:T(2,128)(2,1)S(1)}, u32[]{:S(2)}, u32[]{:S(2)}) %all-to-all-start) | async-done | bytes 196640 | tf_op jit(solution)/shard_map/all_to_all | solution.py:67
  22.4 2.5 %collective-permute-start = (bf16[16,3072]{1,0:T(8,128)(2,1)S(1)}, bf16[16,3072]{1,0:T(8,128)(2,1)S(1)}, u32[]{:S(2)}, u32[]{:S(2)}) collective-permute-start(bf16[16,3072]{1,0:T(8,128)(2,1)S(1)} %get-tuple-element.20), channel_id=1, source_target_pairs={{0,4},{1,5},{2,6},{3,7},{4,0},{5,1},{6,2},{7,3},{8,12},{9,13},{10,... | collective-permute-start | bytes 294920 | tf_op jit(solution)/shard_map/ppermute | solution.py:38
  25.9 2.6 %collective-permute-start.1 = (bf16[32,3072]{1,0:T(8,128)(2,1)S(1)}, bf16[32,3072]{1,0:T(8,128)(2,1)S(1)}, u32[]{:S(2)}, u32[]{:S(2)}) collective-permute-start(bf16[32,3072]{1,0:T(8,128)(2,1)S(1)} %maximum_select_fusion), channel_id=1, source_target_pairs={{0,3},{1,0},{2,1},{3,2},{4,28},{5,29},{6,30},{7,31},{8,11},{9,8},{... | collective-permute-start | bytes 589832 | tf_op jit(solution)/shard_map/ppermute | solution.py:38
  29.7 3.5 %collective-permute-done.1 = bf16[32,3072]{1,0:T(8,128)(2,1)S(1)} collective-permute-done((bf16[32,3072]{1,0:T(8,128)(2,1)S(1)}, bf16[32,3072]{1,0:T(8,128)(2,1)S(1)}, u32[]{:S(2)}, u32[]{:S(2)}) %collective-permute-start.1) | collective-permute-done | bytes 196640 | tf_op jit(solution)/shard_map/ppermute | solution.py:38
  37.0 1.8 %collective-permute-start.9 = (bf16[64,3072]{1,0:T(8,128)(2,1)S(1)}, bf16[64,3072]{1,0:T(8,128)(2,1)S(1)}, u32[]{:S(2)}, u32[]{:S(2)}) collective-permute-start(bf16[64,3072]{1,0:T(8,128)(2,1)S(1)} %get-tuple-element.16), channel_id=1, source_target_pairs={{0,8},{1,9},{2,10},{3,11},{4,5},{5,6},{6,7},{7,4},{8,16},{9,17},{1... | collective-permute-start | bytes 1179656 | tf_op jit(solution)/shard_map/ppermute | solution.py:38
  39.8 3.3 %collective-permute-start.4 = (bf16[128,3072]{1,0:T(8,128)(2,1)S(1)}, bf16[128,3072]{1,0:T(8,128)(2,1)S(1)}, u32[]{:S(2)}, u32[]{:S(2)}) collective-permute-start(bf16[128,3072]{1,0:T(8,128)(2,1)S(1)} %get-tuple-element.15), channel_id=1, source_target_pairs={{0,4},{1,5},{2,6},{3,7},{4,0},{5,1},{6,2},{7,3},{8,12},{9,13},{10,... | collective-permute-start | bytes 2359304 | tf_op jit(solution)/shard_map/ppermute | solution.py:38
  43.0 1.8 %fusion.26 = f32[128,256]{1,0:T(8,128)S(1)} fusion(bf16[128,3072]{1,0:T(8,128)(2,1)S(1)} %get-tuple-element.15, bf16[1,6144,256]{2,1,0:T(8,128)(2,1)} %param.12, s32[]{:T(128)S(6)} %select_n.61), kind=kOutput, calls=%fused_computation.37 | convolution fusion | flops 201326592 | bytes 2490372 | tf_op jit(solution)/shard_map/dot_general | solution.py:118
  48.0 3.6 %collective-permute-start.10 = (bf16[128,3072]{1,0:T(8,128)(2,1)S(1)}, bf16[128,3072]{1,0:T(8,128)(2,1)S(1)}, u32[]{:S(2)}, u32[]{:S(2)}) collective-permute-start(bf16[128,3072]{1,0:T(8,128)(2,1)S(1)} %constant_dynamic-update-slice_fusion.4), channel_id=1, source_target_pairs={{0,4},{1,5},{2,6},{3,7},{4,0},{5,1},{6,2},{7,3},{8,12},{9,13},{10,... | collective-permute-start | bytes 2359304 | tf_op jit(solution)/shard_map/ppermute | solution.py:38
  51.7 2.7 %collective-permute-start.12 = (bf16[64,3072]{1,0:T(8,128)(2,1)S(1)}, bf16[64,3072]{1,0:T(8,128)(2,1)S(1)}, u32[]{:S(2)}, u32[]{:S(2)}) collective-permute-start(bf16[64,3072]{1,0:T(8,128)(2,1)S(1)} %collective-permute-done.6), channel_id=1, source_target_pairs={{0,24},{1,25},{2,26},{3,27},{4,7},{5,4},{6,5},{7,6},{8,0},{9,1},{1... | collective-permute-start | bytes 1179656 | tf_op jit(solution)/shard_map/ppermute | solution.py:38
  55.1 4.7 %collective-permute-done.11 = bf16[64,3072]{1,0:T(8,128)(2,1)S(1)} collective-permute-done((bf16[64,3072]{1,0:T(8,128)(2,1)S(1)}, bf16[64,3072]{1,0:T(8,128)(2,1)S(1)}, u32[]{:S(2)}, u32[]{:S(2)}) %collective-permute-start.11) | collective-permute-done | bytes 393248 | tf_op jit(solution)/shard_map/ppermute | solution.py:38
  60.6 1.6 %collective-permute-start.13 = (bf16[128,3072]{1,0:T(8,128)(2,1)S(1)}, bf16[128,3072]{1,0:T(8,128)(2,1)S(1)}, u32[]{:S(2)}, u32[]{:S(2)}) collective-permute-start(bf16[128,3072]{1,0:T(8,128)(2,1)S(1)} %constant_dynamic-update-slice_fusion.6), channel_id=1, source_target_pairs={{0,4},{1,5},{2,6},{3,7},{4,0},{5,1},{6,2},{7,3},{8,12},{9,13},{10,... | collective-permute-start | bytes 2359304 | tf_op jit(solution)/shard_map/ppermute | solution.py:38
  69.3 2.7 %collective-permute-start.23 = (bf16[64,3072]{1,0:T(8,128)(2,1)S(1)}, bf16[64,3072]{1,0:T(8,128)(2,1)S(1)}, u32[]{:S(2)}, u32[]{:S(2)}) collective-permute-start(bf16[64,3072]{1,0:T(8,128)(2,1)S(1)} %get-tuple-element.8), channel_id=1, source_target_pairs={{0,24},{1,25},{2,26},{3,27},{4,7},{5,4},{6,5},{7,6},{8,0},{9,1},{1... | collective-permute-start | bytes 1179656 | tf_op jit(solution)/shard_map/ppermute | solution.py:38
  74.7 2.0 %collective-permute-done.23 = bf16[64,3072]{1,0:T(8,128)(2,1)S(1)} collective-permute-done((bf16[64,3072]{1,0:T(8,128)(2,1)S(1)}, bf16[64,3072]{1,0:T(8,128)(2,1)S(1)}, u32[]{:S(2)}, u32[]{:S(2)}) %collective-permute-start.23) | collective-permute-done | bytes 393248 | tf_op jit(solution)/shard_map/ppermute | solution.py:38
  76.8 3.2 %collective-permute-start.24 = (bf16[64,3072]{1,0:T(8,128)(2,1)S(1)}, bf16[64,3072]{1,0:T(8,128)(2,1)S(1)}, u32[]{:S(2)}, u32[]{:S(2)}) collective-permute-start(bf16[64,3072]{1,0:T(8,128)(2,1)S(1)} %fusion.79), channel_id=1, source_target_pairs={{0,24},{1,25},{2,26},{3,27},{4,7},{5,4},{6,5},{7,6},{8,0},{9,1},{1... | collective-permute-start | bytes 1179656 | tf_op jit(solution)/shard_map/ppermute | solution.py:38
  81.8 3.3 %collective-permute-done.24 = bf16[64,3072]{1,0:T(8,128)(2,1)S(1)} collective-permute-done((bf16[64,3072]{1,0:T(8,128)(2,1)S(1)}, bf16[64,3072]{1,0:T(8,128)(2,1)S(1)}, u32[]{:S(2)}, u32[]{:S(2)}) %collective-permute-start.24) | collective-permute-done | bytes 393248 | tf_op jit(solution)/shard_map/ppermute | solution.py:38
  85.1 3.2 %collective-permute-done.18 = bf16[64,3072]{1,0:T(8,128)(2,1)S(1)} collective-permute-done((bf16[64,3072]{1,0:T(8,128)(2,1)S(1)}, bf16[64,3072]{1,0:T(8,128)(2,1)S(1)}, u32[]{:S(2)}, u32[]{:S(2)}) %collective-permute-start.18) | collective-permute-done | bytes 393248 | tf_op jit(solution)/shard_map/ppermute | solution.py:38
  88.8 2.8 %collective-permute-start.25 = (bf16[32,3072]{1,0:T(8,128)(2,1)S(1)}, bf16[32,3072]{1,0:T(8,128)(2,1)S(1)}, u32[]{:S(2)}, u32[]{:S(2)}) collective-permute-start(bf16[32,3072]{1,0:T(8,128)(2,1)S(1)} %get-tuple-element.9), channel_id=1, source_target_pairs={{0,3},{1,0},{2,1},{3,2},{4,28},{5,29},{6,30},{7,31},{8,11},{9,8},{... | collective-permute-start | bytes 589832 | tf_op jit(solution)/shard_map/ppermute | solution.py:38
  92.6 1.9 %collective-permute-done.21 = bf16[32,3072]{1,0:T(8,128)(2,1)S(1)} collective-permute-done((bf16[32,3072]{1,0:T(8,128)(2,1)S(1)}, bf16[32,3072]{1,0:T(8,128)(2,1)S(1)}, u32[]{:S(2)}, u32[]{:S(2)}) %collective-permute-start.21) | collective-permute-done | bytes 196640 | tf_op jit(solution)/shard_map/ppermute | solution.py:38
  94.5 1.8 %collective-permute-done.25 = bf16[32,3072]{1,0:T(8,128)(2,1)S(1)} collective-permute-done((bf16[32,3072]{1,0:T(8,128)(2,1)S(1)}, bf16[32,3072]{1,0:T(8,128)(2,1)S(1)}, u32[]{:S(2)}, u32[]{:S(2)}) %collective-permute-start.25) | collective-permute-done | bytes 196640 | tf_op jit(solution)/shard_map/ppermute | solution.py:38
  96.2 1.5 %collective-permute-done.26 = bf16[32,3072]{1,0:T(8,128)(2,1)S(1)} collective-permute-done((bf16[32,3072]{1,0:T(8,128)(2,1)S(1)}, bf16[32,3072]{1,0:T(8,128)(2,1)S(1)}, u32[]{:S(2)}, u32[]{:S(2)}) %collective-permute-start.26) | collective-permute-done | bytes 196640 | tf_op jit(solution)/shard_map/ppermute | solution.py:38
  97.9 4.1 %collective-permute-start.27 = (bf16[16,3072]{1,0:T(8,128)(2,1)S(1)}, bf16[16,3072]{1,0:T(8,128)(2,1)S(1)}, u32[]{:S(2)}, u32[]{:S(2)}) collective-permute-start(bf16[16,3072]{1,0:T(8,128)(2,1)S(1)} %get-tuple-element.14), channel_id=1, source_target_pairs={{0,4},{1,5},{2,6},{3,7},{4,0},{5,1},{6,2},{7,3},{8,12},{9,13},{10,... | collective-permute-start | bytes 294920 | tf_op jit(solution)/shard_map/ppermute | solution.py:38
  103.8 3.4 %all-to-all-start.1 = ((bf16[8,4,3072]{2,1,0:T(4,128)(2,1)}), bf16[8,4,3072]{2,1,0:T(4,128)(2,1)S(1)}, u32[]{:S(2)}, u32[]{:S(2)}) async-start(bf16[8,4,3072]{2,1,0:T(4,128)(2,1)} %pad_maximum_fusion.1), calls=%async_computation.1 | async-start | bytes 393216 | tf_op jit(solution)/shard_map/all_to_all | solution.py:192
  107.4 9.8 %all-to-all-done.1 = bf16[8,4,3072]{2,1,0:T(4,128)(2,1)S(1)} async-done(((bf16[8,4,3072]{2,1,0:T(4,128)(2,1)}), bf16[8,4,3072]{2,1,0:T(4,128)(2,1)S(1)}, u32[]{:S(2)}, u32[]{:S(2)}) %all-to-all-start.1) | async-done | bytes 196640 | tf_op jit(solution)/shard_map/all_to_all | solution.py:192
  (133 shorter events, 32.9 us)
Async XLA Ops:
  4.3 18.0 %all-to-all-start = ((bf16[8,2,6144]{2,1,0:T(2,128)(2,1)}), bf16[8,2,6144]{2,1,0:T(2,128)(2,1)S(1)}, u32[]{:S(2)}, u32[]{:S(2)}) async-start(bf16[8,2,6144]{2,1,0:T(2,128)(2,1)} %reshape.111), calls=%async_computation | async-start | bytes 393216 | tf_op jit(solution)/shard_map/all_to_all | solution.py:67
  25.9 7.3 %collective-permute-start.1 = (bf16[32,3072]{1,0:T(8,128)(2,1)S(1)}, bf16[32,3072]{1,0:T(8,128)(2,1)S(1)}, u32[]{:S(2)}, u32[]{:S(2)}) collective-permute-start(bf16[32,3072]{1,0:T(8,128)(2,1)S(1)} %maximum_select_fusion), channel_id=1, source_target_pairs={{0,3},{1,0},{2,1},{3,2},{4,28},{5,29},{6,30},{7,31},{8,11},{9,8},{... | collective-permute-start | bytes 589832 | tf_op jit(solution)/shard_map/ppermute | solution.py:38
  28.5 8.5 %collective-permute-start.3 = (bf16[32,3072]{1,0:T(8,128)(2,1)S(1)}, bf16[32,3072]{1,0:T(8,128)(2,1)S(1)}, u32[]{:S(2)}, u32[]{:S(2)}) collective-permute-start(bf16[32,3072]{1,0:T(8,128)(2,1)S(1)} %maximum_select_fusion), channel_id=1, source_target_pairs={{0,2},{1,3},{2,0},{3,1},{4,20},{5,21},{6,22},{7,23},{8,10},{9,11},... | collective-permute-start | bytes 589832 | tf_op jit(solution)/shard_map/ppermute | solution.py:38
  29.0 7.9 %collective-permute-start.2 = (bf16[32,3072]{1,0:T(8,128)(2,1)S(1)}, bf16[32,3072]{1,0:T(8,128)(2,1)S(1)}, u32[]{:S(2)}, u32[]{:S(2)}) collective-permute-start(bf16[32,3072]{1,0:T(8,128)(2,1)S(1)} %maximum_select_fusion), channel_id=1, source_target_pairs={{0,1},{1,2},{2,3},{3,0},{4,12},{5,13},{6,14},{7,15},{8,9},{9,10},{... | collective-permute-start | bytes 589832 | tf_op jit(solution)/shard_map/ppermute | solution.py:38
  33.3 14.3 %collective-permute-start.8 = (bf16[64,3072]{1,0:T(8,128)(2,1)S(1)}, bf16[64,3072]{1,0:T(8,128)(2,1)S(1)}, u32[]{:S(2)}, u32[]{:S(2)}) collective-permute-start(bf16[64,3072]{1,0:T(8,128)(2,1)S(1)} %pad_maximum_fusion), channel_id=1, source_target_pairs={{0,8},{1,9},{2,10},{3,11},{4,5},{5,6},{6,7},{7,4},{8,16},{9,17},{1... | collective-permute-start | bytes 1179656 | tf_op jit(solution)/shard_map/ppermute | solution.py:38
  34.6 10.6 %collective-permute-start.5 = (bf16[64,3072]{1,0:T(8,128)(2,1)S(1)}, bf16[64,3072]{1,0:T(8,128)(2,1)S(1)}, u32[]{:S(2)}, u32[]{:S(2)}) collective-permute-start(bf16[64,3072]{1,0:T(8,128)(2,1)S(1)} %pad_maximum_fusion), channel_id=1, source_target_pairs={{0,24},{1,25},{2,26},{3,27},{4,7},{5,4},{6,5},{7,6},{8,0},{9,1},{1... | collective-permute-start | bytes 1179656 | tf_op jit(solution)/shard_map/ppermute | solution.py:38
  37.0 10.5 %collective-permute-start.9 = (bf16[64,3072]{1,0:T(8,128)(2,1)S(1)}, bf16[64,3072]{1,0:T(8,128)(2,1)S(1)}, u32[]{:S(2)}, u32[]{:S(2)}) collective-permute-start(bf16[64,3072]{1,0:T(8,128)(2,1)S(1)} %get-tuple-element.16), channel_id=1, source_target_pairs={{0,8},{1,9},{2,10},{3,11},{4,5},{5,6},{6,7},{7,4},{8,16},{9,17},{1... | collective-permute-start | bytes 1179656 | tf_op jit(solution)/shard_map/ppermute | solution.py:38
  38.8 7.0 %collective-permute-start.6 = (bf16[64,3072]{1,0:T(8,128)(2,1)S(1)}, bf16[64,3072]{1,0:T(8,128)(2,1)S(1)}, u32[]{:S(2)}, u32[]{:S(2)}) collective-permute-start(bf16[64,3072]{1,0:T(8,128)(2,1)S(1)} %get-tuple-element.16), channel_id=1, source_target_pairs={{0,24},{1,25},{2,26},{3,27},{4,7},{5,4},{6,5},{7,6},{8,0},{9,1},{1... | collective-permute-start | bytes 1179656 | tf_op jit(solution)/shard_map/ppermute | solution.py:38
  39.8 22.5 %collective-permute-start.4 = (bf16[128,3072]{1,0:T(8,128)(2,1)S(1)}, bf16[128,3072]{1,0:T(8,128)(2,1)S(1)}, u32[]{:S(2)}, u32[]{:S(2)}) collective-permute-start(bf16[128,3072]{1,0:T(8,128)(2,1)S(1)} %get-tuple-element.15), channel_id=1, source_target_pairs={{0,4},{1,5},{2,6},{3,7},{4,0},{5,1},{6,2},{7,3},{8,12},{9,13},{10,... | collective-permute-start | bytes 2359304 | tf_op jit(solution)/shard_map/ppermute | solution.py:38
  48.0 15.1 %collective-permute-start.10 = (bf16[128,3072]{1,0:T(8,128)(2,1)S(1)}, bf16[128,3072]{1,0:T(8,128)(2,1)S(1)}, u32[]{:S(2)}, u32[]{:S(2)}) collective-permute-start(bf16[128,3072]{1,0:T(8,128)(2,1)S(1)} %constant_dynamic-update-slice_fusion.4), channel_id=1, source_target_pairs={{0,4},{1,5},{2,6},{3,7},{4,0},{5,1},{6,2},{7,3},{8,12},{9,13},{10,... | collective-permute-start | bytes 2359304 | tf_op jit(solution)/shard_map/ppermute | solution.py:38
  51.6 12.3 %collective-permute-start.7 = (bf16[128,3072]{1,0:T(8,128)(2,1)S(1)}, bf16[128,3072]{1,0:T(8,128)(2,1)S(1)}, u32[]{:S(2)}, u32[]{:S(2)}) collective-permute-start(bf16[128,3072]{1,0:T(8,128)(2,1)S(1)} %constant_dynamic-update-slice_fusion.2), channel_id=1, source_target_pairs={{0,4},{1,5},{2,6},{3,7},{4,0},{5,1},{6,2},{7,3},{8,12},{9,13},{10,... | collective-permute-start | bytes 2359304 | tf_op jit(solution)/shard_map/ppermute | solution.py:38
  51.7 8.1 %collective-permute-start.11 = (bf16[64,3072]{1,0:T(8,128)(2,1)S(1)}, bf16[64,3072]{1,0:T(8,128)(2,1)S(1)}, u32[]{:S(2)}, u32[]{:S(2)}) collective-permute-start(bf16[64,3072]{1,0:T(8,128)(2,1)S(1)} %collective-permute-done.8), channel_id=1, source_target_pairs={{0,8},{1,9},{2,10},{3,11},{4,5},{5,6},{6,7},{7,4},{8,16},{9,17},{1... | collective-permute-start | bytes 1179656 | tf_op jit(solution)/shard_map/ppermute | solution.py:38
  51.7 8.2 %collective-permute-start.12 = (bf16[64,3072]{1,0:T(8,128)(2,1)S(1)}, bf16[64,3072]{1,0:T(8,128)(2,1)S(1)}, u32[]{:S(2)}, u32[]{:S(2)}) collective-permute-start(bf16[64,3072]{1,0:T(8,128)(2,1)S(1)} %collective-permute-done.6), channel_id=1, source_target_pairs={{0,24},{1,25},{2,26},{3,27},{4,7},{5,4},{6,5},{7,6},{8,0},{9,1},{1... | collective-permute-start | bytes 1179656 | tf_op jit(solution)/shard_map/ppermute | solution.py:38
  66.7 13.5 %collective-permute-start.14 = (bf16[128,3072]{1,0:T(8,128)(2,1)S(1)}, bf16[128,3072]{1,0:T(8,128)(2,1)S(1)}, u32[]{:S(2)}, u32[]{:S(2)}) collective-permute-start(bf16[128,3072]{1,0:T(8,128)(2,1)S(1)} %convolution_convert_fusion.7), channel_id=1, source_target_pairs={{0,4},{1,5},{2,6},{3,7},{4,0},{5,1},{6,2},{7,3},{8,12},{9,13},{10,... | collective-permute-start | bytes 2359304 | tf_op jit(solution)/shard_map/ppermute | solution.py:38
  69.2 10.8 %collective-permute-start.17 = (bf16[64,3072]{1,0:T(8,128)(2,1)S(1)}, bf16[64,3072]{1,0:T(8,128)(2,1)S(1)}, u32[]{:S(2)}, u32[]{:S(2)}) collective-permute-start(bf16[64,3072]{1,0:T(8,128)(2,1)S(1)} %get-tuple-element.7), channel_id=1, source_target_pairs={{0,8},{1,9},{2,10},{3,11},{4,5},{5,6},{6,7},{7,4},{8,16},{9,17},{1... | collective-permute-start | bytes 1179656 | tf_op jit(solution)/shard_map/ppermute | solution.py:38
  69.3 7.4 %collective-permute-start.23 = (bf16[64,3072]{1,0:T(8,128)(2,1)S(1)}, bf16[64,3072]{1,0:T(8,128)(2,1)S(1)}, u32[]{:S(2)}, u32[]{:S(2)}) collective-permute-start(bf16[64,3072]{1,0:T(8,128)(2,1)S(1)} %get-tuple-element.8), channel_id=1, source_target_pairs={{0,24},{1,25},{2,26},{3,27},{4,7},{5,4},{6,5},{7,6},{8,0},{9,1},{1... | collective-permute-start | bytes 1179656 | tf_op jit(solution)/shard_map/ppermute | solution.py:38
  72.4 8.5 %collective-permute-start.20 = (bf16[64,3072]{1,0:T(8,128)(2,1)S(1)}, bf16[64,3072]{1,0:T(8,128)(2,1)S(1)}, u32[]{:S(2)}, u32[]{:S(2)}) collective-permute-start(bf16[64,3072]{1,0:T(8,128)(2,1)S(1)} %slice.386), channel_id=1, source_target_pairs={{0,24},{1,25},{2,26},{3,27},{4,7},{5,4},{6,5},{7,6},{8,0},{9,1},{1... | collective-permute-start | bytes 1179656 | tf_op jit(solution)/shard_map/ppermute | solution.py:38
  73.4 8.4 %collective-permute-start.22 = (bf16[64,3072]{1,0:T(8,128)(2,1)S(1)}, bf16[64,3072]{1,0:T(8,128)(2,1)S(1)}, u32[]{:S(2)}, u32[]{:S(2)}) collective-permute-start(bf16[64,3072]{1,0:T(8,128)(2,1)S(1)} %slice.385), channel_id=1, source_target_pairs={{0,8},{1,9},{2,10},{3,11},{4,5},{5,6},{6,7},{7,4},{8,16},{9,17},{1... | collective-permute-start | bytes 1179656 | tf_op jit(solution)/shard_map/ppermute | solution.py:38
  76.8 8.3 %collective-permute-start.24 = (bf16[64,3072]{1,0:T(8,128)(2,1)S(1)}, bf16[64,3072]{1,0:T(8,128)(2,1)S(1)}, u32[]{:S(2)}, u32[]{:S(2)}) collective-permute-start(bf16[64,3072]{1,0:T(8,128)(2,1)S(1)} %fusion.79), channel_id=1, source_target_pairs={{0,24},{1,25},{2,26},{3,27},{4,7},{5,4},{6,5},{7,6},{8,0},{9,1},{1... | collective-permute-start | bytes 1179656 | tf_op jit(solution)/shard_map/ppermute | solution.py:38
  80.1 8.2 %collective-permute-start.18 = (bf16[64,3072]{1,0:T(8,128)(2,1)S(1)}, bf16[64,3072]{1,0:T(8,128)(2,1)S(1)}, u32[]{:S(2)}, u32[]{:S(2)}) collective-permute-start(bf16[64,3072]{1,0:T(8,128)(2,1)S(1)} %fusion.82), channel_id=1, source_target_pairs={{0,8},{1,9},{2,10},{3,11},{4,5},{5,6},{6,7},{7,4},{8,16},{9,17},{1... | collective-permute-start | bytes 1179656 | tf_op jit(solution)/shard_map/ppermute | solution.py:38
  88.7 5.8 %collective-permute-start.21 = (bf16[32,3072]{1,0:T(8,128)(2,1)S(1)}, bf16[32,3072]{1,0:T(8,128)(2,1)S(1)}, u32[]{:S(2)}, u32[]{:S(2)}) collective-permute-start(bf16[32,3072]{1,0:T(8,128)(2,1)S(1)} %slice.343), channel_id=1, source_target_pairs={{0,1},{1,2},{2,3},{3,0},{4,12},{5,13},{6,14},{7,15},{8,9},{9,10},{... | collective-permute-start | bytes 589832 | tf_op jit(solution)/shard_map/ppermute | solution.py:38
  88.8 7.5 %collective-permute-start.25 = (bf16[32,3072]{1,0:T(8,128)(2,1)S(1)}, bf16[32,3072]{1,0:T(8,128)(2,1)S(1)}, u32[]{:S(2)}, u32[]{:S(2)}) collective-permute-start(bf16[32,3072]{1,0:T(8,128)(2,1)S(1)} %get-tuple-element.9), channel_id=1, source_target_pairs={{0,3},{1,0},{2,1},{3,2},{4,28},{5,29},{6,30},{7,31},{8,11},{9,8},{... | collective-permute-start | bytes 589832 | tf_op jit(solution)/shard_map/ppermute | solution.py:38
  91.5 6.3 %collective-permute-start.26 = (bf16[32,3072]{1,0:T(8,128)(2,1)S(1)}, bf16[32,3072]{1,0:T(8,128)(2,1)S(1)}, u32[]{:S(2)}, u32[]{:S(2)}) collective-permute-start(bf16[32,3072]{1,0:T(8,128)(2,1)S(1)} %get-tuple-element.10), channel_id=1, source_target_pairs={{0,2},{1,3},{2,0},{3,1},{4,20},{5,21},{6,22},{7,23},{8,10},{9,11},... | collective-permute-start | bytes 589832 | tf_op jit(solution)/shard_map/ppermute | solution.py:38
  103.8 13.4 %all-to-all-start.1 = ((bf16[8,4,3072]{2,1,0:T(4,128)(2,1)}), bf16[8,4,3072]{2,1,0:T(4,128)(2,1)S(1)}, u32[]{:S(2)}, u32[]{:S(2)}) async-start(bf16[8,4,3072]{2,1,0:T(4,128)(2,1)} %pad_maximum_fusion.1), calls=%async_computation.1 | async-start | bytes 393216 | tf_op jit(solution)/shard_map/all_to_all | solution.py:192
  (10 other events, 118.4 us)
